TPU v7x, 32 devices: a whole 2x2x4 slice. The times are simulated.
32 devices in a mesh: node: 8 (over y, x, core), local: 4 (over z).
Axes of the slice: x: 2, y: 2, z: 4, core: 2. Of those that a mesh axis runs over, the one named last changes fastest.
Arguments:
- tokens: bfloat16 [4096, 4096], P(('node', 'local')), may hold values from -6 to 6
- grad_out: bfloat16 [4096, 4096], P(('node', 'local')), may hold values from -6 to 6
- router_logits: float32 [4096, 128], P(('node', 'local')), may hold values from -20 to 280
- group_id: int32 [4096], P(('node', 'local')), may hold values from 0 to 15, as said below
- expert_ids: int32 [4096, 2], P(('node', 'local')), may hold values from 0 to 7, as said below
- w_gate: bfloat16 [8, 4096, 1536], P('node', None, 'local'), may hold values from -0.09375 to 0.09375
- w_up: bfloat16 [8, 4096, 1536], P('node', None, 'local'), may hold values from -0.09375 to 0.09375
- w_down: bfloat16 [8, 1536, 4096], P('node', 'local'), may hold values from -0.15625 to 0.15625
Outputs:
- mixed: bfloat16 [4096, 4096], P(('node', 'local'))
- d_tokens: bfloat16 [4096, 4096], P(('node', 'local'))
- d_logits: float32 [4096, 128], P(('node', 'local'))
- grad_gate: bfloat16 [8, 4096, 1536], P('node', None, 'local')
- grad_up: bfloat16 [8, 4096, 1536], P('node', None, 'local')
- grad_down: bfloat16 [8, 1536, 4096], P('node', 'local')
Inputs may be any that keep to these rules, and one draw needn't show every extreme that they name: `group_id`: A token is computed here when its group is below 1. Among the tokens of one device no expert of those groups is named by more than 6 tokens, and one such expert is named by exactly 6 tokens of every device. `expert_ids`: the two numbers of a token differ; both name experts of the token's group.
All inputs are finite; a program needn't handle non-finite values.
Results may differ from a plain program's by a relative error of at most 0.0065.
Values may be sent and summed in bfloat16 or wider, within the bound.
A program may use at most 192 MiB of HBM per device.

v0:
```python
import jax
import jax.numpy as jnp
from jax import lax
from jax.sharding import PartitionSpec as P

GSIZE = 8
CAP = 6


def gate_weights(logits, group_ids, chosen, inside):
    probabilities = jax.nn.softmax(logits, axis=-1)
    columns = jnp.arange(logits.shape[1], dtype=jnp.int32)
    member = ((columns // GSIZE)[None, :] == group_ids[:, None]).astype(logits.dtype)
    group_mass = jnp.sum(probabilities * member, axis=1)
    picked = jnp.sum(
        jnp.where(chosen[:, :, None] == columns[None, None, :], logits[:, None, :], 0.0), axis=2
    )
    pair_share = jax.nn.softmax(picked, axis=-1)
    return jnp.where(inside[:, None], group_mass[:, None] * pair_share, 0.0)


def spread(buffer):
    arrived = lax.all_to_all(buffer, "node", split_axis=0, concat_axis=2, tiled=True)
    arrived = lax.all_gather(arrived, "local", axis=2, tiled=True)
    return arrived[0]


def collect(partial_sums):
    summed = lax.psum_scatter(partial_sums[None], "local", scatter_dimension=2, tiled=True)
    result = lax.all_to_all(
        summed.astype(jnp.bfloat16), "node", split_axis=2, concat_axis=0, tiled=True
    )
    return result.reshape(-1, result.shape[-1])


def body(tokens, grad_out, router_logits, group_id, expert_ids, w_gate, w_up, w_down):
    owned_count = w_gate.shape[0]
    node_count = lax.axis_size("node")
    expert_total = owned_count * node_count
    window_groups = expert_total // GSIZE
    model_width = tokens.shape[1]
    inside = group_id < window_groups
    chosen = group_id[:, None] * GSIZE + expert_ids
    target = jnp.where(inside[:, None], chosen, expert_total)
    expert_range = jnp.arange(expert_total, dtype=jnp.int32)
    onehot = (target[:, :, None] == expert_range[None, None, :]).astype(jnp.int32)
    per_token = jnp.sum(onehot, axis=1)
    earlier = jnp.cumsum(per_token, axis=0) - per_token
    slot_rank = jnp.sum(onehot * earlier[:, None, :], axis=2)
    slot_index = jnp.where(inside[:, None], target * CAP + slot_rank, -1)
    slot_range = jnp.arange(expert_total * CAP, dtype=jnp.int32)
    first_pick = (slot_range[:, None] == slot_index[None, :, 0]).astype(jnp.bfloat16)
    second_pick = (slot_range[:, None] == slot_index[None, :, 1]).astype(jnp.bfloat16)
    mix_weights, pull_back = jax.vjp(
        lambda values: gate_weights(values, group_id, chosen, inside), router_logits
    )
    grad_f32 = grad_out.astype(jnp.float32)
    first_grad = (mix_weights[:, 0:1] * grad_f32).astype(jnp.bfloat16)
    second_grad = (mix_weights[:, 1:2] * grad_f32).astype(jnp.bfloat16)
    send_rows = (
        jnp.dot(first_pick, tokens, preferred_element_type=jnp.float32)
        + jnp.dot(second_pick, tokens, preferred_element_type=jnp.float32)
    ).astype(jnp.bfloat16)
    send_grads = (
        jnp.dot(first_pick, first_grad, preferred_element_type=jnp.float32)
        + jnp.dot(second_pick, second_grad, preferred_element_type=jnp.float32)
    ).astype(jnp.bfloat16)
    buffer_shape = (node_count, owned_count, CAP, model_width)
    rows_in = spread(send_rows.reshape(buffer_shape))
    gate_pre = jnp.einsum("erd,edf->erf", rows_in, w_gate, preferred_element_type=jnp.float32)
    up_pre = jnp.einsum("erd,edf->erf", rows_in, w_up, preferred_element_type=jnp.float32)
    sigmoid_gate = jax.nn.sigmoid(gate_pre)
    activated = gate_pre * sigmoid_gate
    hidden = (activated * up_pre).astype(jnp.bfloat16)
    partial_out = jnp.einsum("erf,efd->erd", hidden, w_down, preferred_element_type=jnp.float32)
    out_flat = collect(partial_out)
    grads_in = spread(send_grads.reshape(buffer_shape))
    grad_hidden = jnp.einsum("erd,efd->erf", grads_in, w_down, preferred_element_type=jnp.float32)
    grad_gate_pre = (
        grad_hidden * up_pre * sigmoid_gate * (1.0 + gate_pre * (1.0 - sigmoid_gate))
    ).astype(jnp.bfloat16)
    grad_up_pre = (grad_hidden * activated).astype(jnp.bfloat16)
    partial_in = jnp.einsum(
        "erf,edf->erd", grad_gate_pre, w_gate, preferred_element_type=jnp.float32
    ) + jnp.einsum("erf,edf->erd", grad_up_pre, w_up, preferred_element_type=jnp.float32)
    back_flat = collect(partial_in)
    grad_gate = jnp.einsum(
        "erd,erf->edf", rows_in, grad_gate_pre, preferred_element_type=jnp.float32
    ).astype(jnp.bfloat16)
    grad_up = jnp.einsum(
        "erd,erf->edf", rows_in, grad_up_pre, preferred_element_type=jnp.float32
    ).astype(jnp.bfloat16)
    grad_down = jnp.einsum(
        "erf,erd->efd", hidden, grads_in, preferred_element_type=jnp.float32
    ).astype(jnp.bfloat16)
    first_out = jnp.einsum("st,sd->td", first_pick, out_flat, preferred_element_type=jnp.float32)
    second_out = jnp.einsum("st,sd->td", second_pick, out_flat, preferred_element_type=jnp.float32)
    first_back = jnp.einsum("st,sd->td", first_pick, back_flat, preferred_element_type=jnp.float32)
    second_back = jnp.einsum(
        "st,sd->td", second_pick, back_flat, preferred_element_type=jnp.float32
    )
    mixed = (mix_weights[:, 0:1] * first_out + mix_weights[:, 1:2] * second_out).astype(
        jnp.bfloat16
    )
    d_tokens = (first_back + second_back).astype(jnp.bfloat16)
    scores = jnp.stack(
        [jnp.sum(grad_f32 * first_out, axis=1), jnp.sum(grad_f32 * second_out, axis=1)], axis=1
    )
    d_logits = pull_back(scores)[0]
    return (mixed, d_tokens, d_logits, grad_gate, grad_up, grad_down)


def solution(mesh):
    return jax.shard_map(
        body,
        mesh=mesh,
        in_specs=(
            P(("node", "local"), None),
            P(("node", "local"), None),
            P(("node", "local"), None),
            P(("node", "local")),
            P(("node", "local"), None),
            P("node", None, "local"),
            P("node", None, "local"),
            P("node", "local", None),
        ),
        out_specs=(
            P(("node", "local"), None),
            P(("node", "local"), None),
            P(("node", "local"), None),
            P("node", None, "local"),
            P("node", None, "local"),
            P("node", "local", None),
        ),
        check_vma=False,
    )
```

profile of v0, /device:TPU:0, one launch (start us, length us, event | category | flops | bytes accessed | tf_op | source)
XLA Modules:
  0.0 320.4 jit_solution(9817088539204725255)
XLA Ops:
  7.2 0.8 broadcast_compare_fusion
  8.0 0.8 broadcast_multiply_fusion
  8.8 0.7 broadcast_select_fusion
  9.5 0.1 copy.34
  9.6 0.2 reduce_window_sum.11
  9.9 1.6 fusion.51
  11.5 0.3 fusion.5
  11.8 0.9 reshape.170
  12.7 15.0 %all_to_all.42 = bf16[8,1,6,4096]{3,2,1,0:T(8,128)(2,1)} all-to-all(bf16[8,1,6,4096]{3,2,1,0:T(8,128)(2,1)} %bitcast.93), channel_id=1, replica_groups=mesh['node'=8,'local'=4] {'node'}, dimensions={0} | all-to-all | bytes 786432 | tf_op jit(solution)/shard_map/all_to_all | solution.py:23
  27.7 1.9 all_to_all.13
  29.7 36.8 %all-gather.3.cloned.1.call-done = bf16[1,1,192,4096]{3,2,1,0:T(8,128)(2,1)} async-done(((bf16[1,1,48,4096]{3,2,1,0:T(8,128)(2,1)}), bf16[1,1,192,4096]{3,2,1,0:T(8,128)(2,1)}) %all-gather.3.cloned.1.call-update) | async-done | bytes 1572880 | tf_op jit(solution)/shard_map/all_gather | solution.py:24
  66.5 3.5 %fusion.15 = f32[192,384]{1,0:T(8,128)S(1)} fusion(bf16[1,4096,384]{2,1,0:T(8,128)(2,1)} %param.13, bf16[1,1,192,4096]{3,2,1,0:T(8,128)(2,1)} %all-gather.3.cloned.1.call-done), kind=kOutput, calls=%fused_computation.27 | convolution fusion | flops 603979776 | bytes 5013504 | tf_op jit(solution)/shard_map/erd,edf->erf/dot_general | solution.py:70
  70.0 0.3 copy-done.10
  70.3 1.7 multiply_convert_fusion.2
  72.0 0.6 copy-done.13
  72.6 2.7 convolution_bitcast_fusion
  75.3 0.8 copy-done.9
  76.1 0.2 select_reduce_fusion.1
  76.4 0.5 multiply_divide_fusion.1
  76.9 57.9 %reduce-scatter.3.cloned.1.call-done = f32[1,1,48,4096]{3,2,1,0:T(8,128)} async-done(((f32[1,1,192,4096]{3,2,1,0:T(8,128)}), f32[1,1,48,4096]{3,2,1,0:T(8,128)}) %reduce-scatter.3.cloned.1.call-update) | async-done | bytes 786448 | tf_op jit(solution)/shard_map/reduce_scatter | solution.py:29
  134.8 1.2 convert_element_type.66
  135.9 1.7 copy.64
  137.7 0.6 broadcast.90
  138.3 4.9 %reduce = bf16[48,4096]{1,0:T(8,128)(2,1)} reduce(bf16[48,1,1,4096]{3,2,1,0:T(2,128)(2,1)} %bitcast.87, bf16[]{:T(256)} %broadcast.90), dimensions={1,2}, to_apply=%bitcast.86.reduce_sub_computation | reduce | bytes 786434
  143.1 2.1 reshape.179
  145.2 4.1 %all-to-all-start.1 = ((bf16[8,2,12288]{2,1,0:T(2,128)(2,1)}), bf16[8,2,12288]{2,1,0:T(2,128)(2,1)}, u32[]{:S(2)}, u32[]{:S(2)}) async-start(bf16[8,2,12288]{2,1,0:T(2,128)(2,1)} %reshape.179), calls=%async_computation.2 | async-start | bytes 786432 | tf_op jit(solution)/shard_map/all_to_all | solution.py:30
  149.3 0.5 and_select_fusion
  149.9 0.1 reduce_max.18
  150.0 0.2 fusion.50
  150.2 0.5 multiply_divide_fusion
  150.7 6.9 %all-to-all-done.1 = bf16[8,2,12288]{2,1,0:T(2,128)(2,1)} async-done(((bf16[8,2,12288]{2,1,0:T(2,128)(2,1)}), bf16[8,2,12288]{2,1,0:T(2,128)(2,1)}, u32[]{:S(2)}, u32[]{:S(2)}) %all-to-all-start.1) | async-done | bytes 393248 | tf_op jit(solution)/shard_map/all_to_all | solution.py:30
  157.6 3.4 %reshape.180 = bf16[48,1,1,4096]{3,2,1,0:T(2,128)(2,1)} reshape(bf16[8,2,12288]{2,1,0:T(2,128)(2,1)} %all-to-all-done.1) | data formatting | bytes 786432
  161.0 2.0 fusion.35
  163.1 2.2 fusion.19
  165.3 0.7 fusion.49
  166.1 1.2 add_multiply_fusion
  167.3 0.4 fusion.28
  167.7 1.2 fusion.6
  168.9 1.9 reshape.176
  170.8 13.8 %all_to_all.43 = bf16[8,1,6,4096]{3,2,1,0:T(8,128)(2,1)} all-to-all(bf16[8,1,6,4096]{3,2,1,0:T(8,128)(2,1)} %bitcast.94), channel_id=1, replica_groups=mesh['node'=8,'local'=4] {'node'}, dimensions={0} | all-to-all | bytes 786432 | tf_op jit(solution)/shard_map/all_to_all | solution.py:23
  184.6 1.9 all_to_all.16
  186.6 0.2 reduce-scatter.5.cloned.1.call-start
  186.8 35.0 %all-gather.5.cloned.1.call-done = bf16[1,1,192,4096]{3,2,1,0:T(8,128)(2,1)} async-done(((bf16[1,1,48,4096]{3,2,1,0:T(8,128)(2,1)}), bf16[1,1,192,4096]{3,2,1,0:T(8,128)(2,1)}) %all-gather.5.cloned.1.call-update) | async-done | bytes 1572880 | tf_op jit(solution)/shard_map/all_gather | solution.py:24
  221.8 2.8 multiply_convert_fusion
  224.7 1.2 fusion.13
  225.9 0.7 copy-done.7
  226.6 2.9 fusion
  229.6 0.6 copy-done.24
  230.2 0.1 select_reduce_fusion
  230.4 0.8 fusion.46
  231.2 3.8 %add_convert_fusion = bf16[128,4096]{1,0:T(8,128)(2,1)} fusion(f32[128,4096]{1,0:T(8,128)} %copy-done.1, f32[128,4096]{1,0:T(8,128)} %get-tuple-element.24, f32[128]{0:T(128)S(1)} %get-tuple-element.19, f32[128]{0:T(128)S(1)} %get-tuple-element.18), kind=kLoop, calls=%fused_computation.33 | loop fusion | flops 2097152 | bytes 5243904 | tf_op jit(solution)/shard_map/convert_element_type | solution.py:102
  234.9 3.0 fusion.1
  237.9 51.1 %reduce-scatter.5.cloned.1.call-done = f32[1,1,48,4096]{3,2,1,0:T(8,128)} async-done(((f32[1,1,192,4096]{3,2,1,0:T(8,128)}), f32[1,1,48,4096]{3,2,1,0:T(8,128)}) %reduce-scatter.5.cloned.1.call-update) | async-done | bytes 786448 | tf_op jit(solution)/shard_map/reduce_scatter | solution.py:29
  289.0 1.2 convert_element_type.74
  290.2 1.7 copy.63
  291.9 4.1 %reduce.1 = bf16[48,4096]{1,0:T(8,128)(2,1)S(1)} reduce(bf16[48,1,1,4096]{3,2,1,0:T(2,128)(2,1)} %bitcast.88, bf16[]{:T(256)} %broadcast.90), dimensions={1,2}, to_apply=%bitcast.85.reduce_sub_computation | reduce | bytes 786434
  296.0 1.1 reshape.181
  297.1 3.7 %all-to-all-start.3 = ((bf16[8,2,12288]{2,1,0:T(2,128)(2,1)}), bf16[8,2,12288]{2,1,0:T(2,128)(2,1)S(1)}, u32[]{:S(2)}, u32[]{:S(2)}) async-start(bf16[8,2,12288]{2,1,0:T(2,128)(2,1)} %reshape.181), calls=%async_computation.5 | async-start | bytes 786432 | tf_op jit(solution)/shard_map/all_to_all | solution.py:30
  300.8 4.3 %fusion.3 = bf16[1,384,4096]{2,1,0:T(8,128)(2,1)} fusion(bf16[192,384]{1,0:T(8,128)(2,1)} %copy-done.13, bf16[1,1,192,4096]{3,2,1,0:T(8,128)(2,1)} %all-gather.5.cloned.1.call-done), kind=kOutput, calls=%fused_computation.7 | convolution fusion | flops 605552640 | bytes 4866048 | tf_op jit(solution)/shard_map/erf,erd->efd/dot_general | solution.py:93
  305.1 3.0 fusion.2
  308.1 1.0 all-to-all-done.3
  309.1 1.1 reshape.182
  310.2 1.9 fusion.33
  312.1 1.7 fusion.4
  (69 shorter events, 0.6 us)
Async XLA Ops:
  7.2 65.5 %copy-start = (bf16[1,384,4096]{2,1,0:T(8,128)(2,1)S(1)}, bf16[1,384,4096]{2,1,0:T(8,128)(2,1)}, u32[]{:S(2)}) copy-start(bf16[1,384,4096]{2,1,0:T(8,128)(2,1)} %param.15) | copy-start | bytes 9437188
  7.2 59.3 %all-gather.3.cloned.1.call-start = ((), (), s32[]{:S(2)}) async-start(), calls=%async_computation.6 | async-start | bytes 1966080 | tf_op jit(solution)/shard_map/all_gather | solution.py:24
  9.8 1.7 copy-start.4
  29.7 105.1 %reduce-scatter.3.cloned.1.call-start = ((), (), s32[]{:S(2)}) async-start(), calls=%async_computation.7 | async-start | bytes 3932160 | tf_op jit(solution)/shard_map/reduce_scatter | solution.py:29
  66.5 3.5 %copy-start.6 = (bf16[1,4096,384]{2,1,0:T(8,128)(2,1)S(1)}, bf16[1,4096,384]{2,1,0:T(8,128)(2,1)}, u32[]{:S(2)}) copy-start(bf16[1,4096,384]{2,1,0:T(8,128)(2,1)} %param.14) | copy-start | bytes 9437188
  66.5 3.8 %copy-start.10 = (bf16[1,1,192,4096]{3,2,1,0:T(8,128)(2,1)S(1)}, bf16[1,1,192,4096]{3,2,1,0:T(8,128)(2,1)}, u32[]{:S(2)}) copy-start(bf16[1,1,192,4096]{3,2,1,0:T(8,128)(2,1)} %all-gather.3.cloned.1.call-done) | copy-start | bytes 4718596
  72.0 0.6 copy-start.13
  75.3 0.8 copy-start.9
  76.4 88.9 %copy-start.18 = (f32[128]{0:T(128)}, f32[128]{0:T(128)S(1)}, u32[]{:S(2)}) copy-start(f32[128]{0:T(128)S(1)} %fusion.60) | copy-start | bytes 1540
  145.2 12.4 %all-to-all-start.1 = ((bf16[8,2,12288]{2,1,0:T(2,128)(2,1)}), bf16[8,2,12288]{2,1,0:T(2,128)(2,1)}, u32[]{:S(2)}, u32[]{:S(2)}) async-start(bf16[8,2,12288]{2,1,0:T(2,128)(2,1)} %reshape.179), calls=%async_computation.2 | async-start | bytes 786432 | tf_op jit(solution)/shard_map/all_to_all | solution.py:30
  149.3 72.5 %all-gather.5.cloned.1.call-start = ((), (), s32[]{:S(2)}) async-start(), calls=%async_computation.8 | async-start | bytes 1966080 | tf_op jit(solution)/shard_map/all_gather | solution.py:24
  161.0 2.0 copy-start.3
  161.0 2.0 copy-start.5
  163.0 2.2 copy-start.1
  163.0 2.3 copy-start.20
  163.0 2.2 copy-start.22
  163.1 2.2 copy-start.25
  163.1 3.0 copy-start.26
  186.6 102.5 %reduce-scatter.5.cloned.1.call-start = ((), (), s32[]{:S(2)}) async-start(), calls=%async_computation.9 | async-start | bytes 3932160 | tf_op jit(solution)/shard_map/reduce_scatter | solution.py:29
  221.8 2.8 copy-start.2
  224.6 1.3 copy-start.14
  224.6 1.3 copy-start.16
  224.7 2.0 copy-start.7
  229.6 0.6 copy-start.24
  229.6 0.7 copy-start.19
  229.6 0.8 copy-start.21
  229.6 0.8 copy-start.23
  231.2 3.8 %copy-start.11 = (bf16[1,1,192,4096]{3,2,1,0:T(8,128)(2,1)S(1)}, bf16[1,1,192,4096]{3,2,1,0:T(8,128)(2,1)}, u32[]{:S(2)}) copy-start(bf16[1,1,192,4096]{3,2,1,0:T(8,128)(2,1)} %all-gather.3.cloned.1.call-done) | copy-start | bytes 4718596
  231.2 3.8 %copy-start.15 = (bf16[192,384]{1,0:T(8,128)(2,1)S(1)}, bf16[192,384]{1,0:T(8,128)(2,1)}, u32[]{:S(2)}) copy-start(bf16[192,384]{1,0:T(8,128)(2,1)} %copy-done.14) | copy-start | bytes 442372
  297.1 12.0 %all-to-all-start.3 = ((bf16[8,2,12288]{2,1,0:T(2,128)(2,1)}), bf16[8,2,12288]{2,1,0:T(2,128)(2,1)S(1)}, u32[]{:S(2)}, u32[]{:S(2)}) async-start(bf16[8,2,12288]{2,1,0:T(2,128)(2,1)} %reshape.181), calls=%async_computation.5 | async-start | bytes 786432 | tf_op jit(solution)/shard_map/all_to_all | solution.py:30
  300.8 4.3 %copy-start.12 = (bf16[1,1,192,4096]{3,2,1,0:T(8,128)(2,1)S(1)}, bf16[1,1,192,4096]{3,2,1,0:T(8,128)(2,1)}, u32[]{:S(2)}) copy-start(bf16[1,1,192,4096]{3,2,1,0:T(8,128)(2,1)} %all-gather.3.cloned.1.call-done) | copy-start | bytes 4718596
  300.8 4.3 %copy-start.17 = (bf16[192,384]{1,0:T(8,128)(2,1)S(1)}, bf16[192,384]{1,0:T(8,128)(2,1)}, u32[]{:S(2)}) copy-start(bf16[192,384]{1,0:T(8,128)(2,1)} %copy-done.16) | copy-start | bytes 442372
  310.2 1.9 copy-start.8
Sparse Core Ops, SparseCore 0:
  29.8 36.6 all-gather.2
  75.4 59.2 reduce-scatter.2
  186.7 35.0 all-gather.4
  229.7 59.2 reduce-scatter.4
where the time goes:
time: 321 us; the launch traced here: 320 us
  waiting for transfers between devices  189 us (59%)
  matrix products  36.2 us (11%)
  blocking collectives  28.8 us (9%)
  other arithmetic  22.5 us (7%)
  local copies, waits for them, and re-layouts  21.8 us (7%)
  between operations  14.1 us (4%)
  starting transfers between devices  8.09 us (3%)
    reduce_scatter x2, waiting for transfers between devices, collect(): lax.psum_scatter(partial_sums[None], 'local', scatter_dimension=2, tiled=...  109 us
    all_gather x2, waiting for transfers between devices, spread(): arrived = lax.all_gather(arrived, 'local', axis=2, tiled=True)  71.8 us
    all_to_all x2, blocking collectives, spread(): lax.all_to_all(buffer, 'node', split_axis=0, concat_axis=2, tiled=True)  28.8 us
    unnamed x59, local copies, waits for them, and re-layouts  11.5 us
    unnamed x2, other arithmetic  8.97 us
    all_to_all x2, waiting for transfers between devices, collect(): lax.all_to_all(summed.astype(jnp.bfloat16), 'node', split_axis=2, concat_...  7.99 us
    all_to_all x2, starting transfers between devices, collect(): lax.all_to_all(summed.astype(jnp.bfloat16), 'node', split_axis=2, concat_...  7.75 us
  transfers between devices with their start and end apart: 6, of which 6 were waited for; matrix products, arithmetic and copies ran while one was open for 5% of the time, Pallas kernels for 0%

commit v1 on v0

v1 whole, which is shorter than its diff:
```python
import functools

import jax
import jax.numpy as jnp
from jax import lax
from jax.experimental import pallas as pl
from jax.experimental.pallas import tpu as pltpu
from jax.sharding import PartitionSpec as P

GSIZE = 8
CAP = 6
CHUNKS = 4
MESH = pl.DeviceIdType.MESH
F32 = jnp.float32
BF16 = jnp.bfloat16


def greet(n, z, node_count, local_count):
    barrier = pltpu.get_barrier_semaphore()
    for k in range(1, local_count):
        peer = lax.rem(z + k, local_count)
        pl.semaphore_signal(barrier, inc=1, device_id=(n, peer), device_id_type=MESH)
    for k in range(1, node_count):
        peer = lax.rem(n + k, node_count)
        pl.semaphore_signal(barrier, inc=1, device_id=(peer, z), device_id_type=MESH)
    pl.semaphore_wait(barrier, local_count + node_count - 2)


def split(value):
    high = value.astype(BF16)
    return high, (value - high.astype(F32)).astype(BF16)


def one_hots(meta, columns):
    lanes = lax.broadcasted_iota(jnp.int32, (meta.shape[0], columns), 1).astype(F32)
    return lanes == meta[:, 0:1], lanes == meta[:, 1:2]


def dispatch_kernel(
    node_count, local_count, rows, uniques,
    x_ref, meta_ref, out_ref, zmeta_ref,
    zbuf, sendbuf, high_ref, low_ref,
    zsend, zrecv, msend, mrecv, psend, precv, own_sem, place_sem,
):
    n, z = lax.axis_index("node"), lax.axis_index("local")
    width = x_ref.shape[1]
    step = width // CHUNKS
    own = pltpu.make_async_copy(x_ref, zbuf.at[z], own_sem.at[0])
    own.start()
    own_meta = pltpu.make_async_copy(meta_ref, zmeta_ref.at[z], own_sem.at[1])
    own_meta.start()
    greet(n, z, node_count, local_count)
    meta_copies, z_copies = [], []
    for k in range(1, local_count):
        peer = lax.rem(z + k, local_count)
        copy = pltpu.make_async_remote_copy(
            meta_ref, zmeta_ref.at[z], msend.at[k], mrecv.at[k],
            device_id=(n, peer), device_id_type=MESH)
        copy.start()
        meta_copies.append(copy)
    for c in range(CHUNKS):
        cols = pl.ds(c * step, step)
        for k in range(1, local_count):
            peer = lax.rem(z + k, local_count)
            copy = pltpu.make_async_remote_copy(
                x_ref.at[:, cols], zbuf.at[z, :, cols], zsend.at[c, k], zrecv.at[c, k],
                device_id=(n, peer), device_id_type=MESH)
            copy.start()
            z_copies.append(copy)
    own.wait()
    own_meta.wait()
    for copy in meta_copies:
        copy.wait()
    meta = zmeta_ref[...].reshape(local_count * 2 * uniques, 128)
    hot0, hot1 = one_hots(meta, node_count * 2 * rows)
    is_grad = meta[:, 4:5] > 0.5
    scale0 = jnp.where(is_grad, meta[:, 2:3], 1.0)
    scale1 = jnp.where(is_grad, meta[:, 3:4], 1.0)
    mix = jnp.where(hot0, scale0, 0.0) + jnp.where(hot1, scale1, 0.0)
    high, low = split(mix)
    high_ref[...] = high
    low_ref[...] = low
    p_copies, places = [], []
    for c in range(CHUNKS):
        cols = pl.ds(c * step, step)
        for k in range(1, local_count):
            z_copies[c * (local_count - 1) + k - 1].wait()
        block = zbuf[:, :, cols].reshape(local_count * 2 * uniques, step)
        contract = (((0,), (0,)), ((), ()))
        picked = lax.dot_general(
            high_ref[...], block, contract, preferred_element_type=F32
        ) + lax.dot_general(low_ref[...], block, contract, preferred_element_type=F32)
        sendbuf[:, :, cols] = picked.astype(BF16).reshape(node_count, 2 * rows, step)
        for k in range(1, node_count):
            peer = lax.rem(n + k, node_count)
            copy = pltpu.make_async_remote_copy(
                sendbuf.at[peer, :, cols], out_ref.at[n, :, cols],
                psend.at[c, k], precv.at[c, k],
                device_id=(peer, z), device_id_type=MESH)
            copy.start()
            p_copies.append(copy)
        place = pltpu.make_async_copy(
            sendbuf.at[n, :, cols], out_ref.at[n, :, cols], place_sem.at[c])
        place.start()
        places.append(place)
    for copy in places + p_copies:
        copy.wait()


def combine_kernel(
    node_count, local_count, rows, uniques,
    part_ref, q_ref, zmeta_ref, out_ref, qout_ref,
    pbuf, qbuf, sendbuf, qsend, rbuf, rqbuf, high_ref, low_ref,
    psend, precv, qpsend, qprecv, zsend, zrecv, qzsend, qzrecv, own_sem,
):
    n, z = lax.axis_index("node"), lax.axis_index("local")
    width = part_ref.shape[2]
    step = width // CHUNKS
    own = pltpu.make_async_copy(part_ref.at[n], pbuf.at[n], own_sem.at[0])
    own.start()
    own_q = pltpu.make_async_copy(q_ref.at[n], qbuf.at[n], own_sem.at[1])
    own_q.start()
    greet(n, z, node_count, local_count)
    p_copies, q_copies = [], []
    for k in range(1, node_count):
        peer = lax.rem(n + k, node_count)
        copy = pltpu.make_async_remote_copy(
            q_ref.at[peer], qbuf.at[n], qpsend.at[k], qprecv.at[k],
            device_id=(peer, z), device_id_type=MESH)
        copy.start()
        q_copies.append(copy)
    for c in range(CHUNKS):
        cols = pl.ds(c * step, step)
        for k in range(1, node_count):
            peer = lax.rem(n + k, node_count)
            copy = pltpu.make_async_remote_copy(
                part_ref.at[peer, :, cols], pbuf.at[n, :, cols],
                psend.at[c, k], precv.at[c, k],
                device_id=(peer, z), device_id_type=MESH)
            copy.start()
            p_copies.append(copy)
    meta = zmeta_ref[...].reshape(local_count * 2 * uniques, 128)
    hot0, hot1 = one_hots(meta, node_count * 2 * rows)
    is_grad = meta[:, 4:5] > 0.5
    scale0 = jnp.where(is_grad, 1.0, meta[:, 2:3])
    scale1 = jnp.where(is_grad, 1.0, meta[:, 3:4])
    mix = jnp.where(hot0, scale0, 0.0) + jnp.where(hot1, scale1, 0.0)
    high, low = split(mix)
    high_ref[...] = high
    low_ref[...] = low
    own.wait()
    own_q.wait()
    for copy in q_copies:
        copy.wait()
    q_all = qbuf[...].reshape(node_count * 2 * rows, 128)
    q0 = jnp.dot(jnp.where(hot0, 1.0, 0.0), q_all, preferred_element_type=F32,
                 precision=lax.Precision.HIGHEST)
    q1 = jnp.dot(jnp.where(hot1, 1.0, 0.0), q_all, preferred_element_type=F32,
                 precision=lax.Precision.HIGHEST)
    lane = lax.broadcasted_iota(jnp.int32, q0.shape, 1)
    qsend[...] = jnp.where(lane == 0, q0, q1).reshape(local_count, 2 * uniques, 128)
    z_copies, qz_copies = [], []
    for c in range(CHUNKS):
        cols = pl.ds(c * step, step)
        for k in range(1, node_count):
            p_copies[c * (node_count - 1) + k - 1].wait()
        block = pbuf[:, :, cols].reshape(node_count * 2 * rows, step)
        summed = jnp.dot(high_ref[...], block, preferred_element_type=F32) + jnp.dot(
            low_ref[...], block, preferred_element_type=F32)
        sendbuf[:, :, cols] = summed.astype(BF16).reshape(local_count, 2 * uniques, step)
        for k in range(1, local_count):
            peer = lax.rem(z + k, local_count)
            copy = pltpu.make_async_remote_copy(
                sendbuf.at[peer, :, cols], rbuf.at[k, :, cols],
                zsend.at[c, k], zrecv.at[c, k],
                device_id=(n, peer), device_id_type=MESH)
            copy.start()
            z_copies.append(copy)
            if c == 0:
                copy = pltpu.make_async_remote_copy(
                    qsend.at[peer], rqbuf.at[k], qzsend.at[k], qzrecv.at[k],
                    device_id=(n, peer), device_id_type=MESH)
                copy.start()
                qz_copies.append(copy)
    for copy in qz_copies:
        copy.wait()
    q_total = qsend[z]
    for k in range(1, local_count):
        q_total = q_total + rqbuf[k]
    qout_ref[...] = q_total
    for c in range(CHUNKS):
        cols = pl.ds(c * step, step)
        for k in range(1, local_count):
            z_copies[c * (local_count - 1) + k - 1].wait()
        total = sendbuf[z, :, cols].astype(F32)
        for k in range(1, local_count):
            total = total + rbuf[k, :, cols].astype(F32)
        out_ref[:, cols] = total.astype(BF16)


def vmem(count):
    return [pl.BlockSpec(memory_space=pltpu.VMEM)] * count


def dispatch(x, meta, node_count, local_count, rows, uniques):
    width = x.shape[1]
    dma = pltpu.SemaphoreType.DMA
    shape = (local_count * 2 * uniques, node_count * 2 * rows)
    return pl.pallas_call(
        functools.partial(dispatch_kernel, node_count, local_count, rows, uniques),
        out_shape=(
            jax.ShapeDtypeStruct((node_count, 2 * rows, width), BF16),
            jax.ShapeDtypeStruct((local_count, 2 * uniques, 128), F32),
        ),
        in_specs=vmem(2),
        out_specs=tuple(vmem(2)),
        scratch_shapes=[
            pltpu.VMEM((local_count, 2 * uniques, width), BF16),
            pltpu.VMEM((node_count, 2 * rows, width), BF16),
            pltpu.VMEM(shape, BF16),
            pltpu.VMEM(shape, BF16),
            dma((CHUNKS, local_count)), dma((CHUNKS, local_count)),
            dma((local_count,)), dma((local_count,)),
            dma((CHUNKS, node_count)), dma((CHUNKS, node_count)),
            dma((2,)), dma((CHUNKS,)),
        ],
        compiler_params=pltpu.CompilerParams(
            collective_id=0, has_side_effects=True, vmem_limit_bytes=60 * 2**20),
    )(x, meta)


def combine(parts, q_rows, zmeta, node_count, local_count, rows, uniques):
    width = parts.shape[2]
    dma = pltpu.SemaphoreType.DMA
    shape = (local_count * 2 * uniques, node_count * 2 * rows)
    return pl.pallas_call(
        functools.partial(combine_kernel, node_count, local_count, rows, uniques),
        out_shape=(
            jax.ShapeDtypeStruct((2 * uniques, width), BF16),
            jax.ShapeDtypeStruct((2 * uniques, 128), F32),
        ),
        in_specs=vmem(3),
        out_specs=tuple(vmem(2)),
        scratch_shapes=[
            pltpu.VMEM((node_count, 2 * rows, width), BF16),
            pltpu.VMEM((node_count, 2 * rows, 128), F32),
            pltpu.VMEM((local_count, 2 * uniques, width), BF16),
            pltpu.VMEM((local_count, 2 * uniques, 128), F32),
            pltpu.VMEM((local_count, 2 * uniques, width), BF16),
            pltpu.VMEM((local_count, 2 * uniques, 128), F32),
            pltpu.VMEM(shape, BF16),
            pltpu.VMEM(shape, BF16),
            dma((CHUNKS, node_count)), dma((CHUNKS, node_count)),
            dma((node_count,)), dma((node_count,)),
            dma((CHUNKS, local_count)), dma((CHUNKS, local_count)),
            dma((local_count,)), dma((local_count,)),
            dma((2,)),
        ],
        compiler_params=pltpu.CompilerParams(
            collective_id=1, has_side_effects=True, vmem_limit_bytes=60 * 2**20),
    )(parts, q_rows, zmeta)


def body(tokens, grad_out, router_logits, group_id, expert_ids, w_gate, w_up, w_down):
    owned = w_gate.shape[0]
    node_count = lax.axis_size("node")
    local_count = lax.axis_size("local")
    z = lax.axis_index("local")
    token_count, width = tokens.shape
    expert_total = owned * node_count
    window_groups = expert_total // GSIZE
    slots = owned * CAP
    rows = local_count * slots
    uniques = min(token_count, node_count * slots // 2)

    inside = group_id < window_groups
    chosen = group_id[:, None] * GSIZE + expert_ids
    target = jnp.where(inside[:, None], chosen, expert_total)
    expert_range = jnp.arange(expert_total, dtype=jnp.int32)
    onehot = target[:, :, None] == expert_range[None, None, :]
    per_token = jnp.sum(onehot.astype(F32), axis=1)
    counted = jnp.concatenate([per_token, inside[:, None].astype(F32)], axis=1).astype(BF16)
    order = jnp.arange(token_count, dtype=jnp.int32)
    before = (order[None, :] < order[:, None]).astype(BF16)
    earlier = jnp.dot(before, counted, preferred_element_type=F32)
    slot_rank = jnp.sum(jnp.where(onehot, earlier[:, None, :-1], 0.0), axis=2).astype(jnp.int32)
    unique_rank = earlier[:, -1].astype(jnp.int32)
    picks = (
        (jnp.arange(uniques, dtype=jnp.int32)[:, None] == unique_rank[None, :]) & inside[None, :]
    )
    dest = (target // owned) * (2 * rows) + z * slots + (target % owned) * CAP + slot_rank

    probabilities = jax.nn.softmax(router_logits, axis=-1)
    columns = jnp.arange(router_logits.shape[1], dtype=jnp.int32)
    member = (columns // GSIZE)[None, :] == group_id[:, None]
    mass = jnp.sum(jnp.where(member, probabilities, 0.0), axis=1)
    here = chosen[:, :, None] == columns[None, None, :]
    picked = jnp.sum(jnp.where(here, router_logits[:, None, :], 0.0), axis=2)
    share = jax.nn.softmax(picked, axis=-1)
    weights = jnp.where(inside[:, None], mass[:, None] * share, 0.0)

    pick_bf16 = picks.astype(BF16)
    x = jnp.concatenate(
        [jnp.dot(pick_bf16, tokens, preferred_element_type=F32).astype(BF16),
         jnp.dot(pick_bf16, grad_out, preferred_element_type=F32).astype(BF16)], axis=0)
    facts = jnp.concatenate([dest.astype(F32) + 1.0, weights], axis=1)
    facts = jnp.sum(jnp.where(picks[:, :, None], facts[None], 0.0), axis=1)
    base = facts[:, :2] - 1.0
    moved = jnp.where(base < 0.0, -1.0, base + rows)
    zeros = jnp.zeros((uniques, 1), F32)
    meta = jnp.concatenate(
        [jnp.concatenate([base, facts[:, 2:], zeros], axis=1),
         jnp.concatenate([moved, facts[:, 2:], zeros + 1.0], axis=1)], axis=0)
    meta = jnp.pad(meta, ((0, 0), (0, 123)))

    arrived, zmeta = dispatch(x, meta, node_count, local_count, rows, uniques)

    def by_expert(part):
        part = part.reshape(node_count, local_count, owned, CAP, width)
        return part.transpose(2, 0, 1, 3, 4).reshape(owned, node_count * local_count * CAP, width)

    def by_node(part):
        last = part.shape[-1]
        part = part.reshape(owned, node_count, local_count, CAP, last)
        return part.transpose(1, 2, 0, 3, 4).reshape(node_count, rows, last)

    rows_in = by_expert(arrived[:, :rows])
    grads_in = by_expert(arrived[:, rows:])
    gate_pre = jnp.einsum("erd,edf->erf", rows_in, w_gate, preferred_element_type=F32)
    up_pre = jnp.einsum("erd,edf->erf", rows_in, w_up, preferred_element_type=F32)
    sigmoid_gate = jax.nn.sigmoid(gate_pre)
    activated = gate_pre * sigmoid_gate
    hidden = (activated * up_pre).astype(BF16)
    grad_hidden = jnp.einsum("erd,efd->erf", grads_in, w_down, preferred_element_type=F32)
    grad_gate_pre = (
        grad_hidden * up_pre * sigmoid_gate * (1.0 + gate_pre * (1.0 - sigmoid_gate))
    ).astype(BF16)
    grad_up_pre = (grad_hidden * activated).astype(BF16)
    q_part = jnp.sum(hidden.astype(F32) * grad_hidden, axis=2, keepdims=True)
    partial_out = jnp.einsum("erf,efd->erd", hidden, w_down, preferred_element_type=F32)
    partial_in = jnp.einsum(
        "erf,edf->erd", grad_gate_pre, w_gate, preferred_element_type=F32
    ) + jnp.einsum("erf,edf->erd", grad_up_pre, w_up, preferred_element_type=F32)
    parts = jnp.concatenate(
        [by_node(partial_out.astype(BF16)), by_node(partial_in.astype(BF16))], axis=1)
    q_rows = by_node(jnp.broadcast_to(q_part, q_part.shape[:2] + (128,)))
    q_rows = jnp.concatenate([q_rows, q_rows], axis=1)
    grad_gate = jnp.einsum(
        "erd,erf->edf", rows_in, grad_gate_pre, preferred_element_type=F32).astype(BF16)
    grad_up = jnp.einsum(
        "erd,erf->edf", rows_in, grad_up_pre, preferred_element_type=F32).astype(BF16)
    grad_down = jnp.einsum(
        "erf,erd->efd", hidden, grads_in, preferred_element_type=F32).astype(BF16)

    results, q_unique = combine(parts, q_rows, zmeta, node_count, local_count, rows, uniques)

    mixed = jnp.einsum("ut,ud->td", pick_bf16, results[:uniques],
                       preferred_element_type=F32).astype(BF16)
    d_tokens = jnp.einsum("ut,ud->td", pick_bf16, results[uniques:],
                          preferred_element_type=F32).astype(BF16)
    q = jnp.sum(jnp.where(picks[:, :, None], q_unique[:uniques, None, :2], 0.0), axis=0)
    q_sum = q[:, 0:1] + q[:, 1:2]
    lean = share[:, 1:2] * q[:, 0:1] - share[:, 0:1] * q[:, 1:2]
    inner = jnp.where(member, router_logits, -jnp.inf)
    inner = jax.nn.softmax(inner, axis=-1)
    tilt = here[:, 0].astype(F32) - here[:, 1].astype(F32)
    d_logits = q_sum * (inner - probabilities) + lean * tilt
    return (mixed, d_tokens, d_logits, grad_gate, grad_up, grad_down)


def solution(mesh):
    rows = P(("node", "local"), None)
    return jax.shard_map(
        body,
        mesh=mesh,
        in_specs=(
            rows, rows, rows, P(("node", "local")), rows,
            P("node", None, "local"), P("node", None, "local"), P("node", "local", None),
        ),
        out_specs=(
            rows, rows, rows,
            P("node", None, "local"), P("node", None, "local"), P("node", "local", None),
        ),
        check_vma=False,
    )
```

time: 321 us -> 167 us (0.52)
  waiting for transfers between devices: 189 us -> 0 us
  Pallas kernels: 0 us -> 118 us
  blocking collectives: 28.8 us -> 0 us
  local copies, waits for them, and re-layouts: 21.8 us -> 6.74 us
  between operations: 14.1 us -> 0.88 us
  matrix products: 36.2 us -> 24.9 us
  other arithmetic: 22.5 us -> 14.3 us
  starting transfers between devices: 8.09 us -> 0 us
    pallas_call x0 -> x2, Pallas kernels: none -> 118 us  [the longest x1 59.5 us: combine(): pl.pallas_call(functools.partial(combine_kernel, node_count, local_count,...]
    reduce_scatter x2 -> x0, waiting for transfers between devices: 109 us -> none  [collect(): lax.psum_scatter(partial_sums[None], 'local', scatter_dimension=2, tiled=...]
    all_gather x2 -> x0, waiting for transfers between devices: 71.8 us -> none  [spread(): arrived = lax.all_gather(arrived, 'local', axis=2, tiled=True)]
    all_to_all x2 -> x0, blocking collectives: 28.8 us -> none  [spread(): lax.all_to_all(buffer, 'node', split_axis=0, concat_axis=2, tiled=True)]
    dot_general x15 -> x12, matrix products: 32 us -> 19.1 us  [the longest x1 2.96 us: body(): jnp.einsum('erd,erf->edf', rows_in, grad_up_pre, preferred_element_type=F32)]
    unnamed x59 -> x22, local copies, waits for them, and re-layouts: 11.5 us -> 2.13 us
    unnamed x2 -> x0, other arithmetic: 8.97 us -> none
    all_to_all x2 -> x0, waiting for transfers between devices: 7.99 us -> none  [collect(): lax.all_to_all(summed.astype(jnp.bfloat16), 'node', split_axis=2, concat_...]
  transfers between devices with their start and end apart: 6 -> 0, of which waited for: 6 -> 0; matrix products, arithmetic and copies ran while one was open for 5% -> 0% of each run, Pallas kernels for 0% -> 0%
where the time goes in v1:
time: 167 us; the launch traced here: 165 us
  Pallas kernels  118 us (71%)
  matrix products  24.9 us (15%)
  other arithmetic  14.3 us (9%)
  local copies, waits for them, and re-layouts  6.74 us (4%)
    pallas_call x1, Pallas kernels, combine(): pl.pallas_call(functools.partial(combine_kernel, node_count, local_count,...  59.5 us
    pallas_call x1, Pallas kernels, dispatch(): pl.pallas_call(functools.partial(dispatch_kernel, node_count, local_count...  58.4 us
    dot_general x1, matrix products, body(): jnp.einsum('erd,erf->edf', rows_in, grad_gate_pre, preferred_element_type...  4.51 us

profile of v1, /device:TPU:0, one launch (start us, length us, event | category | flops | bytes accessed | tf_op | source)
XLA Modules:
  0.0 164.7 jit_solution(716836287195591098)
XLA Ops:
  0.6 0.0 copy-start
  0.6 0.8 broadcast_compare_fusion
  1.5 0.8 broadcast_multiply_fusion
  2.3 0.7 broadcast_select_fusion
  2.9 1.0 select_reduce_fusion
  4.0 0.1 fusion.19
  4.2 0.9 reduce_max.27
  5.1 1.0 fusion.23
  6.2 1.6 fusion.22
  7.8 0.6 multiply_select_fusion
  8.4 0.1 select_reduce_fusion.1
  8.5 0.1 maximum_maximum_fusion
  8.6 0.1 copy.22
  8.7 0.6 pad.4.meta_ref
  9.3 1.5 convolution_convert_fusion.7
  10.8 1.5 convolution_convert_fusion.6
  12.2 0.8 pad_maximum_fusion.1.x_ref
  13.0 58.4 %shard_map.127 = (bf16[8,48,4096]{2,1,0:T(8,128)(2,1)}, f32[4,48,128]{2,1,0:T(8,128)}) custom-call(bf16[48,4096]{1,0:T(8,128)(2,1)} %pad_maximum_fusion.1.x_ref, f32[48,128]{1,0:T(8,128)} %pad.4.meta_ref), custom_call_target="tpu_custom_call" | custom-call | tf_op jit(solution)/shard_map/pallas_call | solution.py:209
  71.4 0.0 copy-start.3
  71.4 2.4 %fusion.37 = (bf16[8,24,4096]{2,1,0:T(8,128)(2,1)S(1)}, bf16[8,24,4096]{2,1,0:T(8,128)(2,1)S(1)}) fusion(bf16[8,48,4096]{2,1,0:T(8,128)(2,1)} %get-tuple-element.10), kind=kLoop, calls=%fused_computation.82 | loop fusion | bytes 6291456 | tf_op jit(solution)/shard_map/slice | solution.py:328
  73.8 0.0 copy-start.1
  73.8 0.0 copy-start.5
  73.8 0.0 copy-start.4
  73.8 0.4 copy-done.3
  74.2 1.0 fusion.12
  75.3 1.7 %copy-done.4 = bf16[1,4096,384]{2,1,0:T(8,128)(2,1)S(1)} copy-done((bf16[1,4096,384]{2,1,0:T(8,128)(2,1)S(1)}, bf16[1,4096,384]{2,1,0:T(8,128)(2,1)}, u32[]{:S(2)}) %copy-start.4) | copy-done | bytes 3145752
  76.9 1.0 fusion.8
  77.9 0.0 copy-done.1
  77.9 0.0 copy-done.5
  78.0 0.0 copy-done
  78.0 1.4 multiply_reduce_fusion
  79.3 0.0 copy-start.8
  79.3 1.2 fusion.10
  80.6 0.0 copy-done.8
  80.6 1.3 fusion.3
  81.9 1.0 convolution_convert_fusion.3
  82.9 2.0 %pad_maximum_fusion.part_ref = bf16[8,48,4096]{2,1,0:T(8,128)(2,1)} fusion(bf16[8,24,4096]{2,1,0:T(8,128)(2,1)S(1)} %bitcast.60, bf16[8,24,4096]{2,1,0:T(8,128)(2,1)S(1)} %bitcast.57), kind=kLoop, calls=%fused_computation.13 | loop fusion | flops 6291456 | bytes 6291456 | tf_op jit(solution)/shard_map/concatenate | solution.py:344
  84.9 0.0 copy-start.7
  84.9 0.0 copy-start.10
  84.9 0.1 broadcast_in_dim.142
  85.0 0.1 broadcast_in_dim.143
  85.1 0.7 pad_maximum_fusion.2.q_ref
  85.8 59.5 %shard_map.128 = (bf16[48,4096]{1,0:T(8,128)(2,1)}, f32[48,128]{1,0:T(8,128)}) custom-call(bf16[8,48,4096]{2,1,0:T(8,128)(2,1)} %pad_maximum_fusion.part_ref, f32[8,48,128]{2,1,0:T(8,128)} %pad_maximum_fusion.2.q_ref, f32[4,48,128]{2,1,0:T(8,128)} %get-tuple-element.11.zmeta_ref), custom_call_target="tpu_custom_call" | custom-call | tf_op jit(solution)/shard_map/pallas_call | solution.py:236
  145.3 0.7 slice.56
  146.0 0.6 copy.23
  146.6 0.8 select_reduce_fusion.2
  147.4 0.8 add_bitcast_fusion
  148.1 0.1 iota_compare_fusion
  148.2 0.0 copy-done.7
  148.2 0.0 copy-done.10
  148.3 1.5 fusion.18
  149.7 2.4 %convolution_convert_fusion.4 = bf16[128,4096]{1,0:T(8,128)(2,1)} fusion(bf16[48,4096]{1,0:T(8,128)(2,1)} %get-tuple-element.12, s32[128]{0:T(128)S(1)} %fusion.30, pred[128]{0:T(512)(128)(4,1)S(1)} %get-tuple-element.33), kind=kOutput, calls=%fused_computation.9 | convolution fusion | flops 25696256 | bytes 1245824 | tf_op jit(solution)/shard_map/ut,ud->td/dot_general | solution.py:359
  152.1 2.4 %convolution_convert_fusion.5 = bf16[128,4096]{1,0:T(8,128)(2,1)} fusion(bf16[48,4096]{1,0:T(8,128)(2,1)} %get-tuple-element.12, s32[128]{0:T(128)S(1)} %fusion.30, pred[128]{0:T(512)(128)(4,1)S(1)} %get-tuple-element.33), kind=kOutput, calls=%fused_computation.10 | convolution fusion | flops 25696256 | bytes 1245824 | tf_op jit(solution)/shard_map/ut,ud->td/dot_general | solution.py:357
  154.5 0.0 copy-start.2
  154.5 0.0 copy-start.9
  154.5 4.5 %fusion = bf16[1,4096,384]{2,1,0:T(8,128)(2,1)} fusion(bf16[192,4096]{1,0:T(8,128)(2,1)} %bitcast.55, bf16[192,384]{1,0:T(8,128)(2,1)S(1)} %get-tuple-element.26), kind=kOutput, calls=%fused_computation.4 | convolution fusion | flops 605552640 | bytes 4866048 | tf_op jit(solution)/shard_map/erd,erf->edf/dot_general | solution.py:348
  159.0 0.0 copy-done.2
  159.0 0.0 copy-done.9
  159.0 0.0 copy-start.6
  159.0 3.0 %fusion.1 = bf16[1,4096,384]{2,1,0:T(8,128)(2,1)} fusion(bf16[192,4096]{1,0:T(8,128)(2,1)S(1)} %bitcast.56, bf16[192,384]{1,0:T(8,128)(2,1)S(1)} %copy-done.9), kind=kOutput, calls=%fused_computation.5 | convolution fusion | flops 605552640 | bytes 4866048 | tf_op jit(solution)/shard_map/erd,erf->edf/dot_general | solution.py:350
  162.0 0.0 copy-done.6
  162.0 2.7 %fusion.2 = bf16[1,384,4096]{2,1,0:T(8,128)(2,1)} fusion(bf16[192,384]{1,0:T(8,128)(2,1)S(1)} %get-tuple-element.19, bf16[192,4096]{1,0:T(8,128)(2,1)S(1)} %bitcast.59), kind=kOutput, calls=%fused_computation.6 | convolution fusion | flops 605552640 | bytes 4866048 | tf_op jit(solution)/shard_map/erf,erd->efd/dot_general | solution.py:352
  (12 shorter events, 0.1 us)
Async XLA Ops:
  0.6 77.3 %copy-start = (bf16[1,384,4096]{2,1,0:T(8,128)(2,1)S(1)}, bf16[1,384,4096]{2,1,0:T(8,128)(2,1)}, u32[]{:S(2)}) copy-start(bf16[1,384,4096]{2,1,0:T(8,128)(2,1)} %param.15) | copy-start | bytes 9437188
  71.4 2.8 %copy-start.3 = (bf16[1,4096,384]{2,1,0:T(8,128)(2,1)S(1)}, bf16[1,4096,384]{2,1,0:T(8,128)(2,1)}, u32[]{:S(2)}) copy-start(bf16[1,4096,384]{2,1,0:T(8,128)(2,1)} %param.13) | copy-start | bytes 9437188
  73.8 4.1 %copy-start.1 = (bf16[8,24,4096]{2,1,0:T(8,128)(2,1)}, bf16[8,24,4096]{2,1,0:T(8,128)(2,1)S(1)}, u32[]{:S(2)}) copy-start(bf16[8,24,4096]{2,1,0:T(8,128)(2,1)S(1)} %get-tuple-element.25) | copy-start | bytes 4718596
  73.8 4.1 %copy-start.5 = (bf16[8,24,4096]{2,1,0:T(8,128)(2,1)}, bf16[8,24,4096]{2,1,0:T(8,128)(2,1)S(1)}, u32[]{:S(2)}) copy-start(bf16[8,24,4096]{2,1,0:T(8,128)(2,1)S(1)} %get-tuple-element.24) | copy-start | bytes 4718596
  73.8 3.1 %copy-start.4 = (bf16[1,4096,384]{2,1,0:T(8,128)(2,1)S(1)}, bf16[1,4096,384]{2,1,0:T(8,128)(2,1)}, u32[]{:S(2)}) copy-start(bf16[1,4096,384]{2,1,0:T(8,128)(2,1)} %param.14) | copy-start | bytes 9437188
  79.3 1.3 copy-start.8
  84.9 63.3 %copy-start.7 = (f32[128,128]{1,0:T(8,128)S(1)}, f32[128,128]{1,0:T(8,128)}, u32[]{:S(2)}) copy-start(f32[128,128]{1,0:T(8,128)} %param.10) | copy-start | bytes 196612
  84.9 63.3 %copy-start.10 = (s32[128]{0:T(128)S(1)}, s32[128]{0:T(128)}, u32[]{:S(2)}) copy-start(s32[128]{0:T(128)} %param.11) | copy-start | bytes 1540
  154.5 4.5 %copy-start.2 = (bf16[8,24,4096]{2,1,0:T(8,128)(2,1)S(1)}, bf16[8,24,4096]{2,1,0:T(8,128)(2,1)}, u32[]{:S(2)}) copy-start(bf16[8,24,4096]{2,1,0:T(8,128)(2,1)} %copy-done.1) | copy-start | bytes 4718596
  154.5 4.5 %copy-start.9 = (bf16[192,384]{1,0:T(8,128)(2,1)S(1)}, bf16[192,384]{1,0:T(8,128)(2,1)}, u32[]{:S(2)}) copy-start(bf16[192,384]{1,0:T(8,128)(2,1)} %copy-done.8) | copy-start | bytes 442372
  159.0 3.0 %copy-start.6 = (bf16[8,24,4096]{2,1,0:T(8,128)(2,1)S(1)}, bf16[8,24,4096]{2,1,0:T(8,128)(2,1)}, u32[]{:S(2)}) copy-start(bf16[8,24,4096]{2,1,0:T(8,128)(2,1)} %copy-done.5) | copy-start | bytes 4718596

commit v2 on v1

--- a/solution.py
+++ b/solution.py
@@ -10,6 +10,7 @@
 GSIZE = 8
 CAP = 6
 CHUNKS = 4
+FUSED_CHUNKS = 8
 MESH = pl.DeviceIdType.MESH
 F32 = jnp.float32
 BF16 = jnp.bfloat16
@@ -261,58 +262,272 @@
     )(parts, q_rows, zmeta)
 
 
-def body(tokens, grad_out, router_logits, group_id, expert_ids, w_gate, w_up, w_down):
-    owned = w_gate.shape[0]
-    node_count = lax.axis_size("node")
-    local_count = lax.axis_size("local")
-    z = lax.axis_index("local")
-    token_count, width = tokens.shape
-    expert_total = owned * node_count
-    window_groups = expert_total // GSIZE
-    slots = owned * CAP
-    rows = local_count * slots
-    uniques = min(token_count, node_count * slots // 2)
-
-    inside = group_id < window_groups
-    chosen = group_id[:, None] * GSIZE + expert_ids
-    target = jnp.where(inside[:, None], chosen, expert_total)
-    expert_range = jnp.arange(expert_total, dtype=jnp.int32)
-    onehot = target[:, :, None] == expert_range[None, None, :]
-    per_token = jnp.sum(onehot.astype(F32), axis=1)
-    counted = jnp.concatenate([per_token, inside[:, None].astype(F32)], axis=1).astype(BF16)
-    order = jnp.arange(token_count, dtype=jnp.int32)
-    before = (order[None, :] < order[:, None]).astype(BF16)
-    earlier = jnp.dot(before, counted, preferred_element_type=F32)
-    slot_rank = jnp.sum(jnp.where(onehot, earlier[:, None, :-1], 0.0), axis=2).astype(jnp.int32)
-    unique_rank = earlier[:, -1].astype(jnp.int32)
-    picks = (
-        (jnp.arange(uniques, dtype=jnp.int32)[:, None] == unique_rank[None, :]) & inside[None, :]
-    )
-    dest = (target // owned) * (2 * rows) + z * slots + (target % owned) * CAP + slot_rank
-
-    probabilities = jax.nn.softmax(router_logits, axis=-1)
-    columns = jnp.arange(router_logits.shape[1], dtype=jnp.int32)
-    member = (columns // GSIZE)[None, :] == group_id[:, None]
-    mass = jnp.sum(jnp.where(member, probabilities, 0.0), axis=1)
-    here = chosen[:, :, None] == columns[None, None, :]
-    picked = jnp.sum(jnp.where(here, router_logits[:, None, :], 0.0), axis=2)
-    share = jax.nn.softmax(picked, axis=-1)
-    weights = jnp.where(inside[:, None], mass[:, None] * share, 0.0)
-
-    pick_bf16 = picks.astype(BF16)
-    x = jnp.concatenate(
-        [jnp.dot(pick_bf16, tokens, preferred_element_type=F32).astype(BF16),
-         jnp.dot(pick_bf16, grad_out, preferred_element_type=F32).astype(BF16)], axis=0)
-    facts = jnp.concatenate([dest.astype(F32) + 1.0, weights], axis=1)
-    facts = jnp.sum(jnp.where(picks[:, :, None], facts[None], 0.0), axis=1)
-    base = facts[:, :2] - 1.0
-    moved = jnp.where(base < 0.0, -1.0, base + rows)
-    zeros = jnp.zeros((uniques, 1), F32)
-    meta = jnp.concatenate(
-        [jnp.concatenate([base, facts[:, 2:], zeros], axis=1),
-         jnp.concatenate([moved, facts[:, 2:], zeros + 1.0], axis=1)], axis=0)
-    meta = jnp.pad(meta, ((0, 0), (0, 123)))
-
+def layer_kernel(
+    node_count, local_count, rows, uniques, chunks,
+    x_ref, meta_ref, gate_hbm, up_hbm, down_hbm,
+    arrived_ref, hidden_ref, dgate_ref, dup_ref, out_ref, qout_ref,
+    zmeta, zbuf, sendbuf, high_ref, low_ref, back_high, back_low,
+    gate_ref, up_ref, down_ref, gate_acc, up_acc, down_acc,
+    parts, pbuf, q_rows, qbuf, sums, qsums, rbuf, rqbuf,
+    zsend, zrecv, msend, mrecv, psend, precv, psend2, precv2, zsend2, zrecv2,
+    qsend, qrecv, qsend2, qrecv2, own_sem, place_sem, weight_sem,
+):
+    n, z = lax.axis_index("node"), lax.axis_index("local")
+    width = x_ref.shape[1]
+    step = width // chunks
+    total_rows = node_count * 2 * rows
+    total_uniques = local_count * 2 * uniques
+
+    def cols(c):
+        return pl.ds(pl.multiple_of(c * step, step), step)
+
+    def remote(src, dst, send, recv, device):
+        return pltpu.make_async_remote_copy(
+            src, dst, send, recv, device_id=device, device_id_type=MESH)
+
+    def z_peer(k):
+        return lax.rem(z + k, local_count)
+
+    def n_peer(k):
+        return lax.rem(n + k, node_count)
+
+    def z_copy(c, k):
+        return remote(x_ref.at[:, cols(c)], zbuf.at[z, :, cols(c)],
+                      zsend.at[c, k], zrecv.at[c, k], (n, z_peer(k)))
+
+    def p_copy(c, k):
+        return remote(sendbuf.at[n_peer(k), :, cols(c)], arrived_ref.at[n, :, cols(c)],
+                      psend.at[c, k], precv.at[c, k], (n_peer(k), z))
+
+    def place(c):
+        return pltpu.make_async_copy(
+            sendbuf.at[n, :, cols(c)], arrived_ref.at[n, :, cols(c)], place_sem.at[c])
+
+    def p_copy2(c, k):
+        return remote(parts.at[n_peer(k), :, cols(c)], pbuf.at[n, :, cols(c)],
+                      psend2.at[c, k], precv2.at[c, k], (n_peer(k), z))
+
+    def place2(c):
+        return pltpu.make_async_copy(
+            parts.at[n, :, cols(c)], pbuf.at[n, :, cols(c)], place_sem.at[chunks + c])
+
+    def z_copy2(c, k):
+        return remote(sums.at[z_peer(k), :, cols(c)], rbuf.at[k, :, cols(c)],
+                      zsend2.at[c, k], zrecv2.at[c, k], (n, z_peer(k)))
+
+    weights = [
+        pltpu.make_async_copy(gate_hbm, gate_ref, weight_sem.at[0]),
+        pltpu.make_async_copy(up_hbm, up_ref, weight_sem.at[1]),
+        pltpu.make_async_copy(down_hbm, down_ref, weight_sem.at[2]),
+    ]
+    own = pltpu.make_async_copy(x_ref, zbuf.at[z], own_sem.at[0])
+    own.start()
+    own_meta = pltpu.make_async_copy(meta_ref, zmeta.at[z], own_sem.at[1])
+    own_meta.start()
+    greet(n, z, node_count, local_count)
+    meta_copies = [
+        remote(meta_ref, zmeta.at[z], msend.at[k], mrecv.at[k], (n, z_peer(k)))
+        for k in range(1, local_count)
+    ]
+    for copy in meta_copies:
+        copy.start()
+
+    @pl.loop(0, chunks)
+    def _(c):
+        for k in range(1, local_count):
+            z_copy(c, k).start()
+
+    for copy in weights:
+        copy.start()
+    gate_acc[...] = jnp.zeros_like(gate_acc)
+    up_acc[...] = jnp.zeros_like(up_acc)
+    down_acc[...] = jnp.zeros_like(down_acc)
+    own.wait()
+    own_meta.wait()
+    for copy in meta_copies:
+        copy.wait()
+    meta = zmeta[...].reshape(total_uniques, 128)
+    hot0, hot1 = one_hots(meta, total_rows)
+    is_grad = meta[:, 4:5] > 0.5
+    w0, w1 = meta[:, 2:3], meta[:, 3:4]
+    mix = jnp.where(hot0, jnp.where(is_grad, w0, 1.0), 0.0) + jnp.where(
+        hot1, jnp.where(is_grad, w1, 1.0), 0.0)
+    high_ref[...], low_ref[...] = split(mix)
+    mix = jnp.where(hot0, jnp.where(is_grad, 1.0, w0), 0.0) + jnp.where(
+        hot1, jnp.where(is_grad, 1.0, w1), 0.0)
+    back_high[...], back_low[...] = split(mix)
+    over_rows = (((0,), (0,)), ((), ()))
+    over_last = (((1,), (1,)), ((), ()))
+
+    def gather(c):
+        for k in range(1, node_count):
+            p_copy(c, k).wait()
+        place(c).wait()
+        block = arrived_ref[:, :, cols(c)].reshape(total_rows, step)
+        gate_acc[...] += jnp.dot(block, gate_ref[cols(c), :], preferred_element_type=F32)
+        up_acc[...] += jnp.dot(block, up_ref[cols(c), :], preferred_element_type=F32)
+        down_acc[...] += lax.dot_general(
+            block, down_ref[:, cols(c)], over_last, preferred_element_type=F32)
+
+    @pl.loop(0, chunks)
+    def _(c):
+        for k in range(1, local_count):
+            z_copy(c, k).wait()
+        block = zbuf[:, :, cols(c)].reshape(total_uniques, step)
+        picked = lax.dot_general(
+            high_ref[...], block, over_rows, preferred_element_type=F32
+        ) + lax.dot_general(low_ref[...], block, over_rows, preferred_element_type=F32)
+        sendbuf[:, :, cols(c)] = picked.astype(BF16).reshape(node_count, 2 * rows, step)
+        for k in range(1, node_count):
+            p_copy(c, k).start()
+        place(c).start()
+
+        @pl.when(c == 0)
+        def _():
+            for copy in weights:
+                copy.wait()
+
+        @pl.when(c > 0)
+        def _():
+            gather(c - 1)
+
+    gather(chunks - 1)
+
+    hidden_units = gate_acc.shape[1]
+
+    def half(acc, kind):
+        whole = acc[...].reshape(node_count, 2 * rows, hidden_units)
+        return whole[:, kind * rows:(kind + 1) * rows].reshape(node_count * rows, hidden_units)
+
+    gate_pre, up_pre, grad_hidden = half(gate_acc, 0), half(up_acc, 0), half(down_acc, 1)
+    sigmoid_gate = jax.nn.sigmoid(gate_pre)
+    activated = gate_pre * sigmoid_gate
+    hidden = (activated * up_pre).astype(BF16)
+    hidden_ref[...] = hidden
+    dgate_ref[...] = (
+        grad_hidden * up_pre * sigmoid_gate * (1.0 + gate_pre * (1.0 - sigmoid_gate))
+    ).astype(BF16)
+    dup_ref[...] = (grad_hidden * activated).astype(BF16)
+    q_part = jnp.sum(hidden.astype(F32) * grad_hidden, axis=1, keepdims=True)
+    q_part = jnp.broadcast_to(q_part, (node_count * rows, 128)).reshape(node_count, rows, 128)
+    q_rows[...] = jnp.concatenate([q_part, q_part], axis=1)
+
+    def return_sums(c):
+        for k in range(1, node_count):
+            p_copy2(c, k).wait()
+        place2(c).wait()
+        block = pbuf[:, :, cols(c)].reshape(total_rows, step)
+        summed = jnp.dot(back_high[...], block, preferred_element_type=F32) + jnp.dot(
+            back_low[...], block, preferred_element_type=F32)
+        sums[:, :, cols(c)] = summed.astype(BF16).reshape(local_count, 2 * uniques, step)
+        for k in range(1, local_count):
+            z_copy2(c, k).start()
+
+    @pl.loop(0, chunks)
+    def _(c):
+        part_out = jnp.dot(hidden_ref[...], down_ref[:, cols(c)], preferred_element_type=F32)
+        part_in = lax.dot_general(
+            dgate_ref[...], gate_ref[cols(c), :], over_last, preferred_element_type=F32
+        ) + lax.dot_general(
+            dup_ref[...], up_ref[cols(c), :], over_last, preferred_element_type=F32)
+        both = jnp.concatenate(
+            [part_out.reshape(node_count, rows, step), part_in.reshape(node_count, rows, step)],
+            axis=1)
+        parts[:, :, cols(c)] = both.astype(BF16)
+        for k in range(1, node_count):
+            p_copy2(c, k).start()
+        place2(c).start()
+
+        @pl.when(c > 0)
+        def _():
+            return_sums(c - 1)
+
+    q_own = pltpu.make_async_copy(q_rows.at[n], qbuf.at[n], own_sem.at[2])
+    q_own.start()
+    q_copies = [
+        remote(q_rows.at[n_peer(k)], qbuf.at[n], qsend.at[k], qrecv.at[k], (n_peer(k), z))
+        for k in range(1, node_count)
+    ]
+    for copy in q_copies:
+        copy.start()
+    return_sums(chunks - 1)
+    q_own.wait()
+    for copy in q_copies:
+        copy.wait()
+    meta = zmeta[...].reshape(total_uniques, 128)
+    hot0, hot1 = one_hots(meta, total_rows)
+    q_all = qbuf[...].reshape(total_rows, 128)
+    q0 = jnp.dot(jnp.where(hot0, 1.0, 0.0), q_all, preferred_element_type=F32,
+                 precision=lax.Precision.HIGHEST)
+    q1 = jnp.dot(jnp.where(hot1, 1.0, 0.0), q_all, preferred_element_type=F32,
+                 precision=lax.Precision.HIGHEST)
+    lane = lax.broadcasted_iota(jnp.int32, q0.shape, 1)
+    qsums[...] = jnp.where(lane == 0, q0, q1).reshape(local_count, 2 * uniques, 128)
+    q_copies = [
+        remote(qsums.at[z_peer(k)], rqbuf.at[k], qsend2.at[k], qrecv2.at[k], (n, z_peer(k)))
+        for k in range(1, local_count)
+    ]
+    for copy in q_copies:
+        copy.start()
+
+    @pl.loop(0, chunks)
+    def _(c):
+        for k in range(1, local_count):
+            z_copy2(c, k).wait()
+        total = sums[z, :, cols(c)].astype(F32)
+        for k in range(1, local_count):
+            total = total + rbuf[k, :, cols(c)].astype(F32)
+        out_ref[:, cols(c)] = total.astype(BF16)
+
+    for copy in q_copies:
+        copy.wait()
+    q_total = qsums[z]
+    for k in range(1, local_count):
+        q_total = q_total + rqbuf[k]
+    qout_ref[...] = q_total
+
+
+def layer(x, meta, gate, up, down, node_count, local_count, rows, uniques, chunks):
+    width, units = gate.shape
+    dma = pltpu.SemaphoreType.DMA
+    shape = (local_count * 2 * uniques, node_count * 2 * rows)
+    by_node = pltpu.VMEM((node_count, 2 * rows, width), BF16)
+    by_node_q = pltpu.VMEM((node_count, 2 * rows, 128), F32)
+    by_local = pltpu.VMEM((local_count, 2 * uniques, width), BF16)
+    by_local_q = pltpu.VMEM((local_count, 2 * uniques, 128), F32)
+    acc = pltpu.VMEM((node_count * 2 * rows, units), F32)
+    small = jax.ShapeDtypeStruct((node_count * rows, units), BF16)
+    node_sem = [dma((chunks, node_count))] * 2
+    local_sem = [dma((chunks, local_count))] * 2
+    return pl.pallas_call(
+        functools.partial(layer_kernel, node_count, local_count, rows, uniques, chunks),
+        out_shape=(
+            jax.ShapeDtypeStruct((node_count, 2 * rows, width), BF16),
+            small, small, small,
+            jax.ShapeDtypeStruct((2 * uniques, width), BF16),
+            jax.ShapeDtypeStruct((2 * uniques, 128), F32),
+        ),
+        in_specs=vmem(2) + [pl.BlockSpec(memory_space=pl.ANY)] * 3,
+        out_specs=tuple(vmem(6)),
+        scratch_shapes=[
+            by_local_q, by_local, by_node,
+            pltpu.VMEM(shape, BF16), pltpu.VMEM(shape, BF16),
+            pltpu.VMEM(shape, BF16), pltpu.VMEM(shape, BF16),
+            pltpu.VMEM((width, units), BF16), pltpu.VMEM((width, units), BF16),
+            pltpu.VMEM((units, width), BF16),
+            acc, acc, acc,
+            by_node, by_node, by_node_q, by_node_q,
+            by_local, by_local_q, by_local, by_local_q,
+        ] + local_sem + [dma((local_count,))] * 2 + node_sem + node_sem + local_sem
+        + [dma((node_count,))] * 2 + [dma((local_count,))] * 2
+        + [dma((3,)), dma((2 * chunks,)), dma((3,))],
+        compiler_params=pltpu.CompilerParams(
+            collective_id=2, has_side_effects=True, vmem_limit_bytes=60 * 2**20),
+    )(x, meta, gate, up, down)
+
+
+def staged(x, meta, w_gate, w_up, w_down, node_count, local_count, rows, uniques):
+    owned, width, _ = w_gate.shape
     arrived, zmeta = dispatch(x, meta, node_count, local_count, rows, uniques)
 
     def by_expert(part):
@@ -353,6 +568,79 @@
         "erf,erd->efd", hidden, grads_in, preferred_element_type=F32).astype(BF16)
 
     results, q_unique = combine(parts, q_rows, zmeta, node_count, local_count, rows, uniques)
+    return results, q_unique, grad_gate, grad_up, grad_down
+
+
+def body(tokens, grad_out, router_logits, group_id, expert_ids, w_gate, w_up, w_down):
+    owned = w_gate.shape[0]
+    node_count = lax.axis_size("node")
+    local_count = lax.axis_size("local")
+    z = lax.axis_index("local")
+    token_count, width = tokens.shape
+    expert_total = owned * node_count
+    window_groups = expert_total // GSIZE
+    slots = owned * CAP
+    rows = local_count * slots
+    uniques = min(token_count, node_count * slots // 2)
+
+    inside = group_id < window_groups
+    chosen = group_id[:, None] * GSIZE + expert_ids
+    target = jnp.where(inside[:, None], chosen, expert_total)
+    expert_range = jnp.arange(expert_total, dtype=jnp.int32)
+    onehot = target[:, :, None] == expert_range[None, None, :]
+    per_token = jnp.sum(onehot.astype(F32), axis=1)
+    counted = jnp.concatenate([per_token, inside[:, None].astype(F32)], axis=1).astype(BF16)
+    order = jnp.arange(token_count, dtype=jnp.int32)
+    before = (order[None, :] < order[:, None]).astype(BF16)
+    earlier = jnp.dot(before, counted, preferred_element_type=F32)
+    slot_rank = jnp.sum(jnp.where(onehot, earlier[:, None, :-1], 0.0), axis=2).astype(jnp.int32)
+    unique_rank = earlier[:, -1].astype(jnp.int32)
+    picks = (
+        (jnp.arange(uniques, dtype=jnp.int32)[:, None] == unique_rank[None, :]) & inside[None, :]
+    )
+    dest = (target // owned) * (2 * rows) + z * slots + (target % owned) * CAP + slot_rank
+
+    probabilities = jax.nn.softmax(router_logits, axis=-1)
+    columns = jnp.arange(router_logits.shape[1], dtype=jnp.int32)
+    member = (columns // GSIZE)[None, :] == group_id[:, None]
+    mass = jnp.sum(jnp.where(member, probabilities, 0.0), axis=1)
+    here = chosen[:, :, None] == columns[None, None, :]
+    picked = jnp.sum(jnp.where(here, router_logits[:, None, :], 0.0), axis=2)
+    share = jax.nn.softmax(picked, axis=-1)
+    weights = jnp.where(inside[:, None], mass[:, None] * share, 0.0)
+
+    pick_bf16 = picks.astype(BF16)
+    x = jnp.concatenate(
+        [jnp.dot(pick_bf16, tokens, preferred_element_type=F32).astype(BF16),
+         jnp.dot(pick_bf16, grad_out, preferred_element_type=F32).astype(BF16)], axis=0)
+    facts = jnp.concatenate([dest.astype(F32) + 1.0, weights], axis=1)
+    facts = jnp.sum(jnp.where(picks[:, :, None], facts[None], 0.0), axis=1)
+    base = facts[:, :2] - 1.0
+    moved = jnp.where(base < 0.0, -1.0, base + rows)
+    zeros = jnp.zeros((uniques, 1), F32)
+    meta = jnp.concatenate(
+        [jnp.concatenate([base, facts[:, 2:], zeros], axis=1),
+         jnp.concatenate([moved, facts[:, 2:], zeros + 1.0], axis=1)], axis=0)
+    meta = jnp.pad(meta, ((0, 0), (0, 123)))
+
+    if owned == 1 and node_count * rows <= 256:
+        arrived, hidden, dgate, dup, results, q_unique = layer(
+            x, meta, w_gate[0], w_up[0], w_down[0],
+            node_count, local_count, rows, uniques, FUSED_CHUNKS)
+        over_rows = (((0,), (0,)), ((), ()))
+        flat = node_count * rows
+        rows_in = arrived[:, :rows].reshape(flat, width)
+        grads_in = arrived[:, rows:].reshape(flat, width)
+
+        def outer(left, right):
+            return lax.dot_general(
+                left, right, over_rows, preferred_element_type=F32).astype(BF16)[None]
+
+        grad_gate, grad_up, grad_down = (
+            outer(rows_in, dgate), outer(rows_in, dup), outer(hidden, grads_in))
+    else:
+        results, q_unique, grad_gate, grad_up, grad_down = staged(
+            x, meta, w_gate, w_up, w_down, node_count, local_count, rows, uniques)
 
     mixed = jnp.einsum("ut,ud->td", pick_bf16, results[:uniques],
                        preferred_element_type=F32).astype(BF16)

time: 167 us -> 135 us (0.81); the launches traced: 165 us -> 135 us
  matrix products: 24.9 us -> 13.4 us
  Pallas kernels: 118 us -> 110 us
  other arithmetic: 14.3 us -> 8.25 us
  local copies, waits for them, and re-layouts: 6.74 us -> 3.11 us
    dot_general x9 -> x3, matrix products: 17.1 us -> 8.62 us  [outer(): lax.dot_general(left, right, over_rows, preferred_element_type=F32)]
    pallas_call x2 -> x1, Pallas kernels: 118 us -> 110 us  [layer(): pl.pallas_call(functools.partial(layer_kernel, node_count, local_count, r...]
    concatenate x2 -> x0, other arithmetic: 2.72 us -> none  [the longest x1 2.02 us: body(): jnp.concatenate([by_node(partial_out.astype(BF16)), by_node(partial_in.as...]
    unnamed x22 -> x16, local copies, waits for them, and re-layouts: 2.13 us -> 0.04 us
where the time goes in v2:
time: 135 us
  Pallas kernels  110 us (81%)
  matrix products  13.4 us (10%)
  other arithmetic  8.25 us (6%)
  local copies, waits for them, and re-layouts  3.11 us (2%)
    pallas_call x1, Pallas kernels, layer(): pl.pallas_call(functools.partial(layer_kernel, node_count, local_count, r...  110 us
    dot_general x3, matrix products, outer(): lax.dot_general(left, right, over_rows, preferred_element_type=F32)  8.62 us

profile of v2, /device:TPU:0, one launch (start us, length us, event | category | flops | bytes accessed | tf_op | source)
XLA Modules:
  0.0 135.1 jit_solution(3411258723460225304)
XLA Ops:
  0.6 0.0 copy-start
  0.6 0.7 broadcast_compare_fusion
  1.4 0.7 broadcast_multiply_fusion
  2.1 0.7 broadcast_select_fusion
  2.7 1.0 select_reduce_fusion
  3.8 0.1 fusion.7
  4.0 0.9 reduce_max.27
  4.9 1.0 fusion.11
  6.0 1.1 fusion.10
  7.1 0.1 select_reduce_fusion.1
  7.2 0.1 maximum_maximum_fusion
  7.3 0.1 copy.22
  7.4 0.6 pad.4.meta_ref
  8.0 0.0 copy-done
  8.0 0.2 convolution_convert_fusion.6
  8.3 1.5 %convolution_convert_fusion.5 = bf16[24,4096]{1,0:T(8,128)(2,1)S(1)} fusion(bf16[128,4096]{1,0:T(8,128)(2,1)} %param.9, s32[128]{0:T(128)S(1)} %fusion.18, pred[128]{0:T(512)(128)(4,1)S(1)} %get-tuple-element.33), kind=kOutput, calls=%fused_computation.8 | convolution fusion | flops 25270272 | bytes 1245824 | tf_op jit(solution)/shard_map/dot_general | solution.py:615
  9.8 0.8 pad_maximum_fusion.x_ref
  10.5 109.5 %shard_map.127 = (bf16[8,48,4096]{2,1,0:T(8,128)(2,1)}, bf16[192,384]{1,0:T(8,128)(2,1)}, bf16[192,384]{1,0:T(8,128)(2,1)}, bf16[192,384]{1,0:T(8,128)(2,1)}, bf...) custom-call(bf16[48,4096]{1,0:T(8,128)(2,1)} %pad_maximum_fusion.x_ref, f32[48,128]{1,0:T(8,128)} %pad.4.meta_ref, ...), custom_call_target="tpu_custom_call" | custom-call | tf_op jit(solution)/shard_map/pallas_call | solution.py:502
  120.1 0.0 copy-start.7
  120.1 2.3 %fusion.25 = (bf16[8,24,4096]{2,1,0:T(8,128)(2,1)S(1)}, bf16[8,24,4096]{2,1,0:T(8,128)(2,1)S(1)}) fusion(bf16[8,48,4096]{2,1,0:T(8,128)(2,1)} %get-tuple-element.14), kind=kLoop, calls=%fused_computation.61 | loop fusion | bytes 6291456 | tf_op jit(solution)/shard_map/slice | solution.py:633
  122.4 0.0 copy-done.7
  122.4 0.0 copy-start.3
  122.4 3.0 %fusion.1 = bf16[1,4096,384]{2,1,0:T(8,128)(2,1)} fusion(bf16[192,4096]{1,0:T(8,128)(2,1)S(1)} %bitcast.35, bf16[192,384]{1,0:T(8,128)(2,1)S(1)} %copy-done.7), kind=kOutput, calls=%fused_computation.4 | convolution fusion | flops 605552640 | bytes 4866048 | tf_op jit(solution)/shard_map/dot_general | solution.py:636
  125.4 0.0 copy-done.3
  125.4 0.0 copy-start.6
  125.4 2.7 %fusion.2 = bf16[1,384,4096]{2,1,0:T(8,128)(2,1)} fusion(bf16[192,384]{1,0:T(8,128)(2,1)S(1)} %copy-done.3, bf16[192,4096]{1,0:T(8,128)(2,1)S(1)} %bitcast.31), kind=kOutput, calls=%fused_computation.5 | convolution fusion | flops 605552640 | bytes 4866048 | tf_op jit(solution)/shard_map/dot_general | solution.py:636
  128.0 0.0 copy-done.6
  128.0 0.0 copy-start.4
  128.0 0.0 copy-start.1
  128.0 0.0 copy-start.5
  128.1 0.0 copy-start.2
  128.1 3.0 %fusion = bf16[1,4096,384]{2,1,0:T(8,128)(2,1)} fusion(bf16[192,4096]{1,0:T(8,128)(2,1)S(1)} %bitcast.36, bf16[192,384]{1,0:T(8,128)(2,1)S(1)} %copy-done.6), kind=kOutput, calls=%fused_computation.3 | convolution fusion | flops 605552640 | bytes 4866048 | tf_op jit(solution)/shard_map/dot_general | solution.py:636
  131.0 0.0 copy-done.4
  131.0 0.1 copy.23
  131.1 0.1 select_reduce_fusion.2
  131.2 0.1 iota_compare_fusion
  131.3 0.0 copy-done.1
  131.3 0.0 copy-done.5
  131.4 0.8 fusion.6
  132.2 0.0 copy-done.2
  132.2 1.5 %convolution_convert_fusion.3 = bf16[128,4096]{1,0:T(8,128)(2,1)} fusion(bf16[48,4096]{1,0:T(8,128)(2,1)S(1)} %copy-done.2, s32[128]{0:T(128)S(1)} %fusion.18, pred[128]{0:T(512)(128)(4,1)S(1)} %get-tuple-element.33), kind=kOutput, calls=%fused_computation.6 | convolution fusion | flops 25696256 | bytes 1246208 | tf_op jit(solution)/shard_map/ut,ud->td/dot_general | solution.py:647
  133.6 1.5 %convolution_convert_fusion.4 = bf16[128,4096]{1,0:T(8,128)(2,1)} fusion(bf16[48,4096]{1,0:T(8,128)(2,1)S(1)} %copy-done.2, s32[128]{0:T(128)S(1)} %fusion.18, pred[128]{0:T(512)(128)(4,1)S(1)} %get-tuple-element.33), kind=kOutput, calls=%fused_computation.7 | convolution fusion | flops 25696256 | bytes 1246208 | tf_op jit(solution)/shard_map/ut,ud->td/dot_general | solution.py:645
  (15 shorter events, 0.2 us)
Async XLA Ops:
  0.6 7.4 %copy-start = (bf16[128,4096]{1,0:T(8,128)(2,1)S(1)}, bf16[128,4096]{1,0:T(8,128)(2,1)}, u32[]{:S(2)}) copy-start(bf16[128,4096]{1,0:T(8,128)(2,1)} %param.8) | copy-start | bytes 3145732
  120.1 2.3 %copy-start.7 = (bf16[192,384]{1,0:T(8,128)(2,1)S(1)}, bf16[192,384]{1,0:T(8,128)(2,1)}, u32[]{:S(2)}) copy-start(bf16[192,384]{1,0:T(8,128)(2,1)} %get-tuple-element.16) | copy-start | bytes 442372
  122.4 3.0 %copy-start.3 = (bf16[192,384]{1,0:T(8,128)(2,1)S(1)}, bf16[192,384]{1,0:T(8,128)(2,1)}, u32[]{:S(2)}) copy-start(bf16[192,384]{1,0:T(8,128)(2,1)} %get-tuple-element.17) | copy-start | bytes 442372
  125.4 2.7 %copy-start.6 = (bf16[192,384]{1,0:T(8,128)(2,1)S(1)}, bf16[192,384]{1,0:T(8,128)(2,1)}, u32[]{:S(2)}) copy-start(bf16[192,384]{1,0:T(8,128)(2,1)} %get-tuple-element.15) | copy-start | bytes 442372
  128.0 3.0 %copy-start.4 = (f32[48,128]{1,0:T(8,128)S(1)}, f32[48,128]{1,0:T(8,128)}, u32[]{:S(2)}) copy-start(f32[48,128]{1,0:T(8,128)} %get-tuple-element.13) | copy-start | bytes 73732
  128.0 3.3 %copy-start.1 = (f32[128,128]{1,0:T(8,128)S(1)}, f32[128,128]{1,0:T(8,128)}, u32[]{:S(2)}) copy-start(f32[128,128]{1,0:T(8,128)} %param.10) | copy-start | bytes 196612
  128.0 3.3 %copy-start.5 = (s32[128]{0:T(128)S(1)}, s32[128]{0:T(128)}, u32[]{:S(2)}) copy-start(s32[128]{0:T(128)} %param.11) | copy-start | bytes 1540
  128.1 4.1 %copy-start.2 = (bf16[48,4096]{1,0:T(8,128)(2,1)S(1)}, bf16[48,4096]{1,0:T(8,128)(2,1)}, u32[]{:S(2)}) copy-start(bf16[48,4096]{1,0:T(8,128)(2,1)} %get-tuple-element.12) | copy-start | bytes 1179652

commit v3 on v2

--- a/solution.py
+++ b/solution.py
@@ -265,7 +265,8 @@
 def layer_kernel(
     node_count, local_count, rows, uniques, chunks,
     x_ref, meta_ref, gate_hbm, up_hbm, down_hbm,
-    arrived_ref, hidden_ref, dgate_ref, dup_ref, out_ref, qout_ref,
+    out_ref, qout_ref, ggate_hbm, gup_hbm, gdown_hbm,
+    arrived_ref, hidden_ref, dgate_ref, dup_ref, ggate_ref, gup_ref, gdown_ref, grad_sem,
     zmeta, zbuf, sendbuf, high_ref, low_ref, back_high, back_low,
     gate_ref, up_ref, down_ref, gate_acc, up_acc, down_acc,
     parts, pbuf, q_rows, qbuf, sums, qsums, rbuf, rqbuf,
@@ -423,6 +424,29 @@
         for k in range(1, local_count):
             z_copy2(c, k).start()
 
+    def grad_copies(c):
+        return [
+            pltpu.make_async_copy(
+                ggate_ref.at[cols(c), :], ggate_hbm.at[cols(c), :], grad_sem.at[0, c]),
+            pltpu.make_async_copy(
+                gup_ref.at[cols(c), :], gup_hbm.at[cols(c), :], grad_sem.at[1, c]),
+            pltpu.make_async_copy(
+                gdown_ref.at[:, cols(c)], gdown_hbm.at[:, cols(c)], grad_sem.at[2, c]),
+        ]
+
+    def weight_grads(c):
+        block = arrived_ref[:, :, cols(c)].astype(F32)
+        rows_in = block[:, :rows].reshape(node_count * rows, step).astype(BF16)
+        grads_in = block[:, rows:].reshape(node_count * rows, step).astype(BF16)
+        ggate_ref[cols(c), :] = lax.dot_general(
+            rows_in, dgate_ref[...], over_rows, preferred_element_type=F32).astype(BF16)
+        gup_ref[cols(c), :] = lax.dot_general(
+            rows_in, dup_ref[...], over_rows, preferred_element_type=F32).astype(BF16)
+        gdown_ref[:, cols(c)] = lax.dot_general(
+            hidden_ref[...], grads_in, over_rows, preferred_element_type=F32).astype(BF16)
+        for copy in grad_copies(c):
+            copy.start()
+
     @pl.loop(0, chunks)
     def _(c):
         part_out = jnp.dot(hidden_ref[...], down_ref[:, cols(c)], preferred_element_type=F32)
@@ -441,6 +465,8 @@
         @pl.when(c > 0)
         def _():
             return_sums(c - 1)
+
+        weight_grads(c)
 
     q_own = pltpu.make_async_copy(q_rows.at[n], qbuf.at[n], own_sem.at[2])
     q_own.start()
@@ -486,6 +512,11 @@
         q_total = q_total + rqbuf[k]
     qout_ref[...] = q_total
 
+    @pl.loop(0, chunks)
+    def _(c):
+        for copy in grad_copies(c):
+            copy.wait()
+
 
 def layer(x, meta, gate, up, down, node_count, local_count, rows, uniques, chunks):
     width, units = gate.shape
@@ -496,20 +527,24 @@
     by_local = pltpu.VMEM((local_count, 2 * uniques, width), BF16)
     by_local_q = pltpu.VMEM((local_count, 2 * uniques, 128), F32)
     acc = pltpu.VMEM((node_count * 2 * rows, units), F32)
-    small = jax.ShapeDtypeStruct((node_count * rows, units), BF16)
+    small = pltpu.VMEM((node_count * rows, units), BF16)
     node_sem = [dma((chunks, node_count))] * 2
     local_sem = [dma((chunks, local_count))] * 2
     return pl.pallas_call(
         functools.partial(layer_kernel, node_count, local_count, rows, uniques, chunks),
         out_shape=(
-            jax.ShapeDtypeStruct((node_count, 2 * rows, width), BF16),
-            small, small, small,
             jax.ShapeDtypeStruct((2 * uniques, width), BF16),
             jax.ShapeDtypeStruct((2 * uniques, 128), F32),
+            jax.ShapeDtypeStruct((width, units), BF16),
+            jax.ShapeDtypeStruct((width, units), BF16),
+            jax.ShapeDtypeStruct((units, width), BF16),
         ),
         in_specs=vmem(2) + [pl.BlockSpec(memory_space=pl.ANY)] * 3,
-        out_specs=tuple(vmem(6)),
+        out_specs=tuple(vmem(2) + [pl.BlockSpec(memory_space=pl.ANY)] * 3),
         scratch_shapes=[
+            by_node, small, small, small,
+            pltpu.VMEM((width, units), BF16), pltpu.VMEM((width, units), BF16),
+            pltpu.VMEM((units, width), BF16), dma((3, chunks)),
             by_local_q, by_local, by_node,
             pltpu.VMEM(shape, BF16), pltpu.VMEM(shape, BF16),
             pltpu.VMEM(shape, BF16), pltpu.VMEM(shape, BF16),
@@ -624,20 +659,10 @@
     meta = jnp.pad(meta, ((0, 0), (0, 123)))
 
     if owned == 1 and node_count * rows <= 256:
-        arrived, hidden, dgate, dup, results, q_unique = layer(
+        results, q_unique, grad_gate, grad_up, grad_down = layer(
             x, meta, w_gate[0], w_up[0], w_down[0],
             node_count, local_count, rows, uniques, FUSED_CHUNKS)
-        over_rows = (((0,), (0,)), ((), ()))
-        flat = node_count * rows
-        rows_in = arrived[:, :rows].reshape(flat, width)
-        grads_in = arrived[:, rows:].reshape(flat, width)
-
-        def outer(left, right):
-            return lax.dot_general(
-                left, right, over_rows, preferred_element_type=F32).astype(BF16)[None]
-
-        grad_gate, grad_up, grad_down = (
-            outer(rows_in, dgate), outer(rows_in, dup), outer(hidden, grads_in))
+        grad_gate, grad_up, grad_down = grad_gate[None], grad_up[None], grad_down[None]
     else:
         results, q_unique, grad_gate, grad_up, grad_down = staged(
             x, meta, w_gate, w_up, w_down, node_count, local_count, rows, uniques)

time: 135 us -> 135 us (level)
  local copies, waits for them, and re-layouts: 3.11 us -> 10.2 us
  matrix products: 13.4 us -> 6.62 us
    unnamed x16 -> x13, local copies, waits for them, and re-layouts: 0.04 us -> 8.73 us
    dot_general x3 -> x0, matrix products: 8.62 us -> none  [outer(): lax.dot_general(left, right, over_rows, preferred_element_type=F32)]
    slice x1 -> x0, local copies, waits for them, and re-layouts: 2.27 us -> none  [body(): grads_in = arrived[:, rows:].reshape(flat, width)]
where the time goes in v3:
time: 135 us
  Pallas kernels  109 us (81%)
  local copies, waits for them, and re-layouts  10.2 us (8%)
  other arithmetic  8.25 us (6%)
  matrix products  6.62 us (5%)
    pallas_call x1, Pallas kernels, layer(): pl.pallas_call(functools.partial(layer_kernel, node_count, local_count, r...  109 us
    unnamed x13, local copies, waits for them, and re-layouts  8.73 us

profile of v3, /device:TPU:0, one launch (start us, length us, event | category | flops | bytes accessed | tf_op | source)
XLA Modules:
  0.0 134.6 jit_solution(12027004061125413778)
XLA Ops:
  0.6 0.0 copy-start
  0.6 0.7 broadcast_compare_fusion
  1.4 0.7 broadcast_multiply_fusion
  2.1 0.7 broadcast_select_fusion
  2.7 1.0 select_reduce_fusion
  3.8 0.1 fusion.4
  4.0 0.9 reduce_max.27
  4.9 1.0 fusion.8
  6.0 1.1 fusion.7
  7.1 0.1 select_reduce_fusion.1
  7.2 0.1 maximum_maximum_fusion
  7.3 0.1 copy.22
  7.4 0.6 pad.4.meta_ref
  8.0 0.0 copy-done
  8.0 0.2 convolution_convert_fusion.3
  8.3 1.5 %convolution_convert_fusion.2 = bf16[24,4096]{1,0:T(8,128)(2,1)S(1)} fusion(bf16[128,4096]{1,0:T(8,128)(2,1)} %param.9, s32[128]{0:T(128)S(1)} %fusion.15, pred[128]{0:T(512)(128)(4,1)S(1)} %get-tuple-element.29), kind=kOutput, calls=%fused_computation.2 | convolution fusion | flops 25270272 | bytes 1245824 | tf_op jit(solution)/shard_map/dot_general | solution.py:650
  9.8 0.8 pad_maximum_fusion.x_ref
  10.5 0.0 copy-start.3
  10.5 0.0 copy-start.4
  10.5 108.7 %shard_map.127 = (bf16[48,4096]{1,0:T(8,128)(2,1)}, f32[48,128]{1,0:T(8,128)}, bf16[4096,384]{1,0:T(8,128)(2,1)}, bf16[4096,384]{1,0:T(8,128)(2,1)}, bf16[384,4096]{1,0:T(8,128)(2,1)}) custom-call(bf16[48,4096]{1,0:T(8,128)(2,1)} %pad_maximum_fusion.x_ref, f32[48,128]{1,0:T(8,128)} %pad.4.meta_ref, bf16[4096,384]{1,0:T(8,128)(2,1)} %bitcast.23, ...), custom_call_target="tpu_custom_call" | custom-call | tf_op jit(solution)/shard_map/pallas_call | solution.py:533
  119.3 0.7 slice.48
  120.0 0.1 copy.23
  120.1 0.1 select_reduce_fusion.2
  120.2 0.1 iota_compare_fusion
  120.3 0.0 copy-done.3
  120.3 0.0 copy-done.4
  120.3 0.8 fusion.3
  121.1 2.4 %convolution_convert_fusion = bf16[128,4096]{1,0:T(8,128)(2,1)} fusion(bf16[48,4096]{1,0:T(8,128)(2,1)} %get-tuple-element.11, s32[128]{0:T(128)S(1)} %fusion.15, pred[128]{0:T(512)(128)(4,1)S(1)} %get-tuple-element.29), kind=kOutput, calls=%fused_computation | convolution fusion | flops 25696256 | bytes 1245824 | tf_op jit(solution)/shard_map/ut,ud->td/dot_general | solution.py:672
  123.5 2.4 %convolution_convert_fusion.1 = bf16[128,4096]{1,0:T(8,128)(2,1)} fusion(bf16[48,4096]{1,0:T(8,128)(2,1)} %get-tuple-element.11, s32[128]{0:T(128)S(1)} %fusion.15, pred[128]{0:T(512)(128)(4,1)S(1)} %get-tuple-element.29), kind=kOutput, calls=%fused_computation.1 | convolution fusion | flops 25696256 | bytes 1245824 | tf_op jit(solution)/shard_map/ut,ud->td/dot_general | solution.py:670
  125.9 0.0 copy-start.2
  125.9 4.0 %copy.27 = bf16[1,4096,384]{2,1,0:T(8,128)(2,1)} copy(bf16[1,4096,384]{2,1,0:T(8,128)(2,1)} %bitcast.22) | data formatting | bytes 6291456
  129.9 0.0 copy-done.2
  129.9 0.0 copy-start.1
  129.9 1.7 %copy.28 = bf16[1,4096,384]{2,1,0:T(8,128)(2,1)} copy(bf16[1,4096,384]{2,1,0:T(8,128)(2,1)S(1)} %bitcast.21) | data formatting | bytes 6291456
  131.6 1.4 %copy-done.1 = bf16[384,4096]{1,0:T(8,128)(2,1)S(1)} copy-done((bf16[384,4096]{1,0:T(8,128)(2,1)S(1)}, bf16[384,4096]{1,0:T(8,128)(2,1)}, u32[]{:S(2)}) %copy-start.1) | copy-done | bytes 3145752
  132.9 1.7 %copy.29 = bf16[1,384,4096]{2,1,0:T(8,128)(2,1)} copy(bf16[1,384,4096]{2,1,0:T(8,128)(2,1)S(1)} %bitcast.20) | data formatting | bytes 6291456
  (14 shorter events, 0.2 us)
Async XLA Ops:
  0.6 7.4 %copy-start = (bf16[128,4096]{1,0:T(8,128)(2,1)S(1)}, bf16[128,4096]{1,0:T(8,128)(2,1)}, u32[]{:S(2)}) copy-start(bf16[128,4096]{1,0:T(8,128)(2,1)} %param.8) | copy-start | bytes 3145732
  10.5 109.8 %copy-start.3 = (f32[128,128]{1,0:T(8,128)S(1)}, f32[128,128]{1,0:T(8,128)}, u32[]{:S(2)}) copy-start(f32[128,128]{1,0:T(8,128)} %param.10) | copy-start | bytes 196612
  10.5 109.8 %copy-start.4 = (s32[128]{0:T(128)S(1)}, s32[128]{0:T(128)}, u32[]{:S(2)}) copy-start(s32[128]{0:T(128)} %param.11) | copy-start | bytes 1540
  125.9 4.0 %copy-start.2 = (bf16[4096,384]{1,0:T(8,128)(2,1)S(1)}, bf16[4096,384]{1,0:T(8,128)(2,1)}, u32[]{:S(2)}) copy-start(bf16[4096,384]{1,0:T(8,128)(2,1)} %get-tuple-element.14) | copy-start | bytes 9437188
  129.9 3.0 %copy-start.1 = (bf16[384,4096]{1,0:T(8,128)(2,1)S(1)}, bf16[384,4096]{1,0:T(8,128)(2,1)}, u32[]{:S(2)}) copy-start(bf16[384,4096]{1,0:T(8,128)(2,1)} %get-tuple-element.15) | copy-start | bytes 9437188
